TPU v7x, 1024 devices: a whole 8x8x8 slice. The times are simulated.
1024 devices in a mesh: gx: 16 (over z_hi, y), gy: 8 (over z_lo, core), gz: 8 (over x).
Axes of the slice: x: 8, y: 8, z: 8 (z_hi: 2, z_lo: 4; z = z_hi * 4 + z_lo), core: 2. Of those that a mesh axis runs over, the one named last changes fastest.
Arguments:
- residual: float32 [128, 256, 1024], P('gx', 'gy', 'gz'), may hold values from -32 to 32
- direction: float32 [128, 256, 1024], P('gx', 'gy', 'gz'), may hold values from -32 to 32
- diagonal: float32 [128, 256, 1024], P('gx', 'gy', 'gz'), may hold values from 0.5 to 2
- recycled: bfloat16 [16, 128, 256, 1024], P(None, 'gx', 'gy', 'gz'), may hold values from -6 to 6
- recycled_images: bfloat16 [16, 128, 256, 1024], P(None, 'gx', 'gy', 'gz'), may hold values from -0.00024414062 to 0.00024414062
- coupling_inverse: float32 [16, 16], replicated, may hold values from -1 to 3, as said below
Outputs:
- solution_delta: float32 [128, 256, 1024], P('gx', 'gy', 'gz')
- new_residual: float32 [128, 256, 1024], P('gx', 'gy', 'gz')
- new_direction: float32 [128, 256, 1024], P('gx', 'gy', 'gz')
Inputs may be any that keep to these rules, and one draw needn't show every extreme that they name: `coupling_inverse`: symmetric.
All inputs are finite; a program needn't handle non-finite values.
Results may differ from a plain program's by a relative error of at most 0.0028.
Values sent between devices are 32-bit elements; how exact they have to be, the bound alone decides.
A program may use at most 32 MiB of HBM per device.

v0:
```python
import jax
import jax.numpy as jnp
import numpy as np
from jax import lax
from jax.sharding import Mesh
from jax.sharding import PartitionSpec as P

S = 4
BASIS = 9
GX_GY_GZ = ("gx_0", "gx_1", "gy_0", "gy_1", "gz")
GX = ("gx_0", "gx_1")
GY = ("gy_0", "gy_1")


center = 7.25
half_width = 6.75


def extended(block, sides, width):
    for axis, dim in sides:
        count = lax.axis_size(axis)
        forward = [(i, i + 1) for i in range(count - 1)]
        forward.append((count - 1, 0))
        backward = [(target, source) for source, target in forward]
        low = lax.ppermute(
            lax.slice_in_dim(block, block.shape[dim] - width, None, axis=dim), axis, forward
        )
        high = lax.ppermute(lax.slice_in_dim(block, 0, width, axis=dim), axis, backward)
        block = jnp.concatenate([low, block, high], axis=dim)
    return block


def by_axis(array, axes):
    for axis in axes:
        array = lax.psum(array, axis)
    return array


def inside(padded):
    centre_cells = padded[:, 1:-1, 1:-1, 1:-1]
    beside_all = padded[:, 2:, 1:-1, 1:-1] + padded[:, :-2, 1:-1, 1:-1]
    beside_all = beside_all + padded[:, 1:-1, 2:, 1:-1] + padded[:, 1:-1, :-2, 1:-1]
    beside_all = beside_all + padded[:, 1:-1, 1:-1, 2:] + padded[:, 1:-1, 1:-1, :-2]
    return (centre_cells, beside_all)


def trim_margin(values, margin):
    if margin == 0:
        return values
    return values[..., margin:-margin, margin:-margin, margin:-margin]


def chebyshev_next(current, beside_all, diagonal, earlier):
    mapped = (6.0 + diagonal) * current - beside_all
    scaled = (mapped - center * current) / half_width
    if earlier is None:
        return scaled
    return 2.0 * scaled - earlier


def recurrence_matrix():
    recurrence = np.zeros((BASIS, BASIS), np.float32)
    for offset, length in ((0, S + 1), (S + 1, S)):
        recurrence[offset, offset] = center
        recurrence[offset + 1, offset] = half_width
        for column in range(1, length - 1):
            recurrence[offset + column + 1, offset + column] = half_width / 2
            recurrence[offset + column, offset + column] = center
            recurrence[offset + column - 1, offset + column] = half_width / 2
    return jnp.asarray(recurrence, dtype=jnp.float32)


def coordinates(totals, coupling_inverse):
    precise = lax.Precision.HIGHEST
    gram_block = totals[:BASIS]
    projections = totals[BASIS:]
    recurrence = recurrence_matrix()
    counter = jnp.arange(BASIS)
    residue = (counter == S + 1).astype(jnp.float32)
    search = (counter == 0).astype(jnp.float32)
    update = jnp.zeros((BASIS,), jnp.float32)
    norm_now = jnp.dot(residue, jnp.dot(gram_block, residue, precision=precise), precision=precise)
    for iteration in range(S):
        mapped = jnp.dot(recurrence, search, precision=precise)
        step_size = norm_now / jnp.dot(
            search, jnp.dot(gram_block, mapped, precision=precise), precision=precise
        )
        update = update + step_size * search
        residue = residue - step_size * mapped
        norm_next = jnp.dot(
            residue, jnp.dot(gram_block, residue, precision=precise), precision=precise
        )
        search = residue + norm_next / norm_now * search
        norm_now = norm_next
    weights = jnp.dot(
        coupling_inverse, jnp.dot(projections, residue, precision=precise), precision=precise
    )
    return (update, residue, search, weights.astype(jnp.bfloat16))


def body(residual, direction, diagonal, recycled, recycled_images, coupling_inverse):
    precise = lax.Precision.HIGHEST
    search_basis = [direction]
    residue_basis = [residual]
    earlier = None
    packed = jnp.stack([direction, residual, diagonal])
    padded = extended(packed, ((GX, 1), (GY, 2), ("gz", 3)), S)
    wide_diag = padded[2]
    current = padded[:2]
    for iteration in range(S):
        if iteration == S - 1:
            current = current[:1]
            earlier = earlier[:1]
        centre_cells, beside_all = inside(current)
        margin = S - iteration - 1
        local_diag = trim_margin(wide_diag, iteration + 1)
        previous = None if earlier is None else trim_margin(earlier, 2)
        following = chebyshev_next(centre_cells, beside_all, local_diag, previous)
        earlier, current = (current, following)
        search_basis.append(trim_margin(following[0], margin))
        if following.shape[0] > 1:
            residue_basis.append(trim_margin(following[1], margin))
    basis = jnp.stack(search_basis + residue_basis)
    basis_flat = basis.reshape(basis.shape[0], -1)
    gram_block = lax.dot_general(
        basis_flat,
        basis_flat,
        (((1,), (1,)), ((), ())),
        precision=precise,
        preferred_element_type=jnp.float32,
    )
    rounded = basis_flat.astype(jnp.bfloat16)
    images = recycled_images.reshape(recycled_images.shape[0], -1)
    projections = lax.dot_general(
        images, rounded, (((1,), (1,)), ((), ())), preferred_element_type=jnp.float32
    )
    totals = by_axis(jnp.concatenate([gram_block, projections], 0), GX_GY_GZ)
    update, residue, search, weights = coordinates(totals, coupling_inverse)
    shape = residual.shape
    solution_delta = jnp.dot(update, basis_flat, precision=precise).reshape(shape)
    new_residual = jnp.dot(residue, basis_flat, precision=precise).reshape(shape)
    correction = jnp.dot(
        weights, recycled.reshape(recycled.shape[0], -1), preferred_element_type=jnp.float32
    )
    new_direction = (jnp.dot(search, basis_flat, precision=precise) - correction).reshape(shape)
    return (solution_delta, new_residual, new_direction)


def solution(mesh):
    split = Mesh(
        mesh.devices.reshape(2, 8, 4, 2, mesh.shape["gz"]), ("gx_0", "gx_1", "gy_0", "gy_1", "gz")
    )
    return jax.shard_map(
        body,
        mesh=split,
        in_specs=(
            P(GX, GY, "gz"),
            P(GX, GY, "gz"),
            P(GX, GY, "gz"),
            P(None, GX, GY, "gz"),
            P(None, GX, GY, "gz"),
            P(),
        ),
        out_specs=(P(GX, GY, "gz"), P(GX, GY, "gz"), P(GX, GY, "gz")),
        check_vma=False,
    )
```

profile of v0, /device:TPU:8, one launch (start us, length us, event | category | flops | bytes accessed | tf_op | source)
XLA Modules:
  0.0 156.8 jit_solution(15243233401220275656)
XLA Ops:
  0.7 1.1 pad_maximum_fusion.2
  1.8 3.6 %collective-permute-start = (f32[3,4,32,128]{3,2,1,0:T(8,128)S(1)}, f32[3,4,32,128]{3,2,1,0:T(8,128)S(1)}, u32[]{:S(2)}, u32[]{:S(2)}) collective-permute-start(f32[3,4,32,128]{3,2,1,0:T(8,128)S(1)} %get-tuple-element.13), channel_id=1, source_target_pairs={{0,64},{64,128},{128,192},{192,256},{256,320},{320,384},{384,448},... | collective-permute-start | bytes 589832 | tf_op jit(solution)/shard_map/ppermute | solution.py:25
  5.4 16.6 %collective-permute-start.1 = (f32[3,4,32,128]{3,2,1,0:T(8,128)S(1)}, f32[3,4,32,128]{3,2,1,0:T(8,128)S(1)}, u32[]{:S(2)}, u32[]{:S(2)}) collective-permute-start(f32[3,4,32,128]{3,2,1,0:T(8,128)S(1)} %get-tuple-element.14), channel_id=1, source_target_pairs={{64,0},{128,64},{192,128},{256,192},{320,256},{384,320},{448,384},... | collective-permute-start | bytes 589832 | tf_op jit(solution)/shard_map/ppermute | solution.py:28
  22.0 5.6 %collective-permute-done = f32[3,4,32,128]{3,2,1,0:T(8,128)S(1)} collective-permute-done((f32[3,4,32,128]{3,2,1,0:T(8,128)S(1)}, f32[3,4,32,128]{3,2,1,0:T(8,128)S(1)}, u32[]{:S(2)}, u32[]{:S(2)}) %collective-permute-start) | collective-permute-done | bytes 196640 | tf_op jit(solution)/shard_map/ppermute | solution.py:25
  27.7 0.9 pad_maximum_fusion.7
  28.6 1.9 %collective-permute-start.2 = (f32[3,16,4,128]{3,2,1,0:T(4,128)S(1)}, f32[3,16,4,128]{3,2,1,0:T(4,128)S(1)}, u32[]{:S(2)}, u32[]{:S(2)}) collective-permute-start(f32[3,16,4,128]{3,2,1,0:T(4,128)S(1)} %get-tuple-element.11), channel_id=1, source_target_pairs={{0,8},{8,16},{16,24},{24,32},{32,40},{40,48},{48,56},{56,0},{1,9},... | collective-permute-start | bytes 294920 | tf_op jit(solution)/shard_map/ppermute | solution.py:25
  30.5 7.5 %collective-permute-start.3 = (f32[3,16,4,128]{3,2,1,0:T(4,128)S(1)}, f32[3,16,4,128]{3,2,1,0:T(4,128)S(1)}, u32[]{:S(2)}, u32[]{:S(2)}) collective-permute-start(f32[3,16,4,128]{3,2,1,0:T(4,128)S(1)} %get-tuple-element.12), channel_id=1, source_target_pairs={{8,0},{16,8},{24,16},{32,24},{40,32},{48,40},{56,48},{0,56},{9,1},... | collective-permute-start | bytes 294920 | tf_op jit(solution)/shard_map/ppermute | solution.py:28
  38.0 0.4 collective-permute-done.2
  38.5 1.7 %collective-permute-done.3 = f32[3,16,4,128]{3,2,1,0:T(4,128)S(1)} collective-permute-done((f32[3,16,4,128]{3,2,1,0:T(4,128)S(1)}, f32[3,16,4,128]{3,2,1,0:T(4,128)S(1)}, u32[]{:S(2)}, u32[]{:S(2)}) %collective-permute-start.3) | collective-permute-done | bytes 98336 | tf_op jit(solution)/shard_map/ppermute | solution.py:28
  40.4 0.3 fusion.105
  40.7 0.4 copy.18
  41.1 2.5 %collective-permute-start.4 = (f32[3,16,40,4]{2,1,3,0:T(8,128)S(1)}, f32[3,16,40,4]{2,1,3,0:T(8,128)S(1)}, u32[]{:S(2)}, u32[]{:S(2)}) collective-permute-start(f32[3,16,40,4]{2,1,3,0:T(8,128)S(1)} %copy.18), channel_id=1, source_target_pairs={{0,1},{1,2},{2,3},{3,4},{4,5},{5,6},{6,7},{7,0},{8,9},{9,10},{10,1... | collective-permute-start | bytes 92168 | tf_op jit(solution)/shard_map/ppermute | solution.py:25
  43.6 0.4 copy.19
  44.0 4.6 %collective-permute-start.5 = (f32[3,16,40,4]{2,1,3,0:T(8,128)S(1)}, f32[3,16,40,4]{2,1,3,0:T(8,128)S(1)}, u32[]{:S(2)}, u32[]{:S(2)}) collective-permute-start(f32[3,16,40,4]{2,1,3,0:T(8,128)S(1)} %copy.19), channel_id=1, source_target_pairs={{1,0},{2,1},{3,2},{4,3},{5,4},{6,5},{7,6},{0,7},{9,8},{10,9},{11,1... | collective-permute-start | bytes 92168 | tf_op jit(solution)/shard_map/ppermute | solution.py:28
  48.8 0.4 copy.20
  49.2 1.5 collective-permute-done.5
  50.7 0.4 copy.21
  51.2 1.1 pad_maximum_fusion
  52.3 0.2 slice_add_fusion.15
  52.9 1.9 %fusion.6 = f32[2,14,38,134]{3,2,1,0:T(8,128)S(1)} fusion(f32[3,16,40,136]{3,2,1,0:T(8,128)S(1)} %pad_maximum_fusion, f32[14,38,134]{2,1,0:T(8,128)S(1)} %slice_add_fusion.15), kind=kLoop, calls=%fused_computation.8 | loop fusion | flops 1425760 | bytes 4847584 | tf_op jit(solution)/shard_map/div | solution.py:55
  54.7 1.9 %slice_subtract_fusion = f32[2,12,36,132]{3,2,1,0:T(8,128)S(1)} fusion(f32[3,16,40,136]{3,2,1,0:T(8,128)S(1)} %pad_maximum_fusion, f32[2,14,38,134]{3,2,1,0:T(8,128)S(1)} %fusion.6, f32[12,36,132]{2,1,0:T(8,128)S(1)} %slice_add_fusion.16), kind=kLoop, calls=%fused_computation.43 | loop fusion | flops 1254528 | bytes 4333824 | tf_op jit(solution)/shard_map/sub | solution.py:58
  56.6 1.6 %slice_subtract_fusion.1 = f32[2,10,34,130]{3,2,1,0:T(8,128)S(1)} fusion(f32[2,14,38,134]{3,2,1,0:T(8,128)S(1)} %fusion.6, f32[2,12,36,132]{3,2,1,0:T(8,128)S(1)} %slice_subtract_fusion, f32[10,34,130]{2,1,0:T(8,128)S(1)} %slice_add_fusion.17), kind=kLoop, calls=%fused_computation.53 | loop fusion | flops 972400 | bytes 3359200 | tf_op jit(solution)/shard_map/sub | solution.py:58
  58.2 0.3 slice_subtract_fusion.2
  59.4 1.9 %stack.65 = f32[9,8,32,128]{3,0,2,1:T(8,128)S(1)} concatenate(f32[1,8,32,128]{3,0,2,1:T(1,128)S(1)} %bitcast.249, f32[1,8,32,128]{3,0,2,1:T(1,128)S(1)} %bitcast.273, f32[1,8,32,128]{3,0,2,1:T(1,128)S(1)} %bitcast.267, f32[1,8,32,128]{3,0,2,1:T(1,128)S(1)} %bitcast.263, f32[1,8,32,128]{3,0,2,1:T(1,128)S(1)} %bitcast.261, f32[1,8,32,128]{3,0,2,1:T(1,128)S(1)} %bitcast.255, ...), dimensions={0} | concatenate | bytes 2359296 | tf_op jit(solution)/shard_map/stack | solution.py:123
  61.3 2.9 %convolution_bitcast_fusion.1 = f32[9,9]{0,1:T(8,128)S(1)} fusion(f32[9,8,32,128]{3,0,2,1:T(8,128)S(1)} %stack.65), kind=kOutput, calls=%fused_computation.14 | convolution fusion | flops 31850496 | bytes 1179972 | tf_op jit(solution)/shard_map/dot_general | solution.py:125
  64.2 1.9 %stack.75 = f32[9,32768]{1,0:T(8,128)S(1)} concatenate(f32[1,32768]{1,0:T(1,128)S(1)} %bitcast.250, f32[1,32768]{1,0:T(1,128)S(1)} %bitcast.274, f32[1,32768]{1,0:T(1,128)S(1)} %bitcast.268, f32[1,32768]{1,0:T(1,128)S(1)} %bitcast.264, f32[1,32768]{1,0:T(1,128)S(1)} %bitcast.262, f32[1,32768]{1,0:T(1,128)S(1)} %bitcast.256, f32[1,32768]{1,0:T(1,128)S(1)} %bitcast.272, ...), dimensions={0} | concatenate | bytes 2359296 | tf_op jit(solution)/shard_map/stack | solution.py:123
  66.1 2.0 %convolution_bitcast_fusion = f32[16,9]{0,1:T(8,128)S(1)} fusion(bf16[2,8,256,128]{3,2,1,0:T(8,128)(2,1)} %bitcast.275, f32[9,32768]{1,0:T(8,128)S(1)} %stack.75), kind=kOutput, calls=%fused_computation.13 | convolution fusion | flops 9732096 | bytes 2228800 | tf_op jit(solution)/shard_map/dot_general | solution.py:134
  68.2 8.9 %psum.35 = f32[25,9]{0,1:T(8,128)S(1)} all-reduce(f32[25,9]{0,1:T(8,128)S(1)} %pad_maximum_fusion.8), channel_id=1, replica_groups=mesh['gx_0'=2,'gx_1'=8,'gy_0'=4,'gy_1'=2,'gz'=8] {'gx_0'}, use_global_device_ids=true, to_apply=%region_0.0 | all-reduce | flops 225 | bytes 1800 | tf_op jit(solution)/shard_map/psum | solution.py:35
  77.1 21.2 %psum.36 = f32[25,9]{0,1:T(8,128)S(1)} all-reduce(f32[25,9]{0,1:T(8,128)S(1)} %psum.35), channel_id=1, replica_groups=mesh['gx_0'=2,'gx_1'=8,'gy_0'=4,'gy_1'=2,'gz'=8] {'gx_1'}, use_global_device_ids=true, to_apply=%region_1.0 | all-reduce | flops 225 | bytes 1800 | tf_op jit(solution)/shard_map/psum | solution.py:35
  98.2 11.8 %psum.37 = f32[25,9]{0,1:T(8,128)S(1)} all-reduce(f32[25,9]{0,1:T(8,128)S(1)} %psum.36), channel_id=1, replica_groups=mesh['gx_0'=2,'gx_1'=8,'gy_0'=4,'gy_1'=2,'gz'=8] {'gy_0'}, use_global_device_ids=true, to_apply=%region_2.0 | all-reduce | flops 225 | bytes 1800 | tf_op jit(solution)/shard_map/psum | solution.py:35
  110.0 2.5 %psum.38 = f32[25,9]{0,1:T(8,128)S(1)} all-reduce(f32[25,9]{0,1:T(8,128)S(1)} %psum.37), channel_id=1, replica_groups=mesh['gx_0'=2,'gx_1'=8,'gy_0'=4,'gy_1'=2,'gz'=8] {'gy_1'}, use_global_device_ids=true, to_apply=%region_3.0 | all-reduce | flops 225 | bytes 1800 | tf_op jit(solution)/shard_map/psum | solution.py:35
  112.5 18.1 %psum.39 = f32[25,9]{0,1:T(8,128)S(1)} all-reduce(f32[25,9]{0,1:T(8,128)S(1)} %psum.38), channel_id=1, replica_groups=mesh['gx_0'=2,'gx_1'=8,'gy_0'=4,'gy_1'=2,'gz'=8] {'gz'}, use_global_device_ids=true, to_apply=%region_4.0 | all-reduce | flops 225 | bytes 1800 | tf_op jit(solution)/shard_map/psum | solution.py:35
  130.6 0.7 fusion.31
  131.3 0.7 fusion.30
  133.4 0.7 fusion.32
  135.6 0.8 fusion.33
  137.7 0.7 fusion.34
  139.9 0.8 fusion.35
  142.0 0.8 fusion.36
  144.4 0.8 fusion.37
  146.5 0.2 convolution_bitcast_fusion.3
  146.7 0.7 fusion.38
  147.5 0.4 copy.55
  148.0 2.4 %fusion = f32[1,8,32,128]{3,0,2,1:T(1,128)} fusion(f32[8,32,128,9]{2,1,0,3:T(8,128)S(1)} %bitcast.242, f32[9]{0:T(128)S(1)} %fusion.67), kind=kOutput, calls=%fused_computation | convolution fusion | flops 3538944 | bytes 1310756 | tf_op jit(solution)/shard_map/dot_general | solution.py:141
  150.4 2.4 %fusion.2 = f32[1,8,32,128]{3,0,2,1:T(1,128)} fusion(f32[8,32,128,9]{2,1,0,3:T(8,128)S(1)} %bitcast.243, f32[9]{0:T(128)S(1)} %multiply_add_fusion, f32[9]{0:T(128)S(1)} %multiply_add_fusion.1, f32[9]{0:T(128)S(1)} %select_add_fusion, f32[]{:T(128)S(6)} %div.44, f32[]{:T(128)S(6)} %div.42, f32[]{:T(128)S(6)} %div.40, f32[]{:T(128)S(6)} %div.38), kind=kOutput, calls=%fused_computation.2 | convolution fusion | flops 3539016 | bytes 1310844 | tf_op jit(solution)/shard_map/dot_general | solution.py:140
  154.2 1.1 fusion.62
  155.4 0.7 fusion.18
  156.1 0.7 sub.63
  (41 shorter events, 2.4 us)
Async XLA Ops:
  0.6 154.7 %copy-start = (f32[16,16]{1,0:T(8,128)S(1)}, f32[16,16]{1,0:T(8,128)}, u32[]{:S(2)}) copy-start(f32[16,16]{1,0:T(8,128)} %param.12) | copy-start | bytes 3076
  0.6 39.6 %copy-start.1 = (f32[8,32,128]{2,1,0:T(8,128)S(1)}, f32[8,32,128]{2,1,0:T(8,128)}, u32[]{:S(2)}) copy-start(f32[8,32,128]{2,1,0:T(8,128)} %param.8) | copy-start | bytes 393220
  0.7 39.6 %copy-start.2 = (f32[8,32,128]{2,1,0:T(8,128)S(1)}, f32[8,32,128]{2,1,0:T(8,128)}, u32[]{:S(2)}) copy-start(f32[8,32,128]{2,1,0:T(8,128)} %param.7) | copy-start | bytes 393220
  0.7 39.6 %copy-start.3 = (f32[8,32,128]{2,1,0:T(8,128)S(1)}, f32[8,32,128]{2,1,0:T(8,128)}, u32[]{:S(2)}) copy-start(f32[8,32,128]{2,1,0:T(8,128)} %param.9) | copy-start | bytes 393220
  1.8 25.8 %collective-permute-start = (f32[3,4,32,128]{3,2,1,0:T(8,128)S(1)}, f32[3,4,32,128]{3,2,1,0:T(8,128)S(1)}, u32[]{:S(2)}, u32[]{:S(2)}) collective-permute-start(f32[3,4,32,128]{3,2,1,0:T(8,128)S(1)} %get-tuple-element.13), channel_id=1, source_target_pairs={{0,64},{64,128},{128,192},{192,256},{256,320},{320,384},{384,448},... | collective-permute-start | bytes 589832 | tf_op jit(solution)/shard_map/ppermute | solution.py:25
  5.4 22.2 %collective-permute-start.1 = (f32[3,4,32,128]{3,2,1,0:T(8,128)S(1)}, f32[3,4,32,128]{3,2,1,0:T(8,128)S(1)}, u32[]{:S(2)}, u32[]{:S(2)}) collective-permute-start(f32[3,4,32,128]{3,2,1,0:T(8,128)S(1)} %get-tuple-element.14), channel_id=1, source_target_pairs={{64,0},{128,64},{192,128},{256,192},{320,256},{384,320},{448,384},... | collective-permute-start | bytes 589832 | tf_op jit(solution)/shard_map/ppermute | solution.py:28
  28.6 9.9 %collective-permute-start.2 = (f32[3,16,4,128]{3,2,1,0:T(4,128)S(1)}, f32[3,16,4,128]{3,2,1,0:T(4,128)S(1)}, u32[]{:S(2)}, u32[]{:S(2)}) collective-permute-start(f32[3,16,4,128]{3,2,1,0:T(4,128)S(1)} %get-tuple-element.11), channel_id=1, source_target_pairs={{0,8},{8,16},{16,24},{24,32},{32,40},{40,48},{48,56},{56,0},{1,9},... | collective-permute-start | bytes 294920 | tf_op jit(solution)/shard_map/ppermute | solution.py:25
  30.5 9.7 %collective-permute-start.3 = (f32[3,16,4,128]{3,2,1,0:T(4,128)S(1)}, f32[3,16,4,128]{3,2,1,0:T(4,128)S(1)}, u32[]{:S(2)}, u32[]{:S(2)}) collective-permute-start(f32[3,16,4,128]{3,2,1,0:T(4,128)S(1)} %get-tuple-element.12), channel_id=1, source_target_pairs={{8,0},{16,8},{24,16},{32,24},{40,32},{48,40},{56,48},{0,56},{9,1},... | collective-permute-start | bytes 294920 | tf_op jit(solution)/shard_map/ppermute | solution.py:28
  40.7 7.9 %copy-start.5 = (f32[9,9]{1,0:T(8,128)S(1)}, f32[9,9]{1,0:T(8,128)}, u32[]{:S(2)}) copy-start(f32[9,9]{1,0:T(8,128)} %constant.17.clone) | copy-start | bytes 976
  41.1 7.7 %collective-permute-start.4 = (f32[3,16,40,4]{2,1,3,0:T(8,128)S(1)}, f32[3,16,40,4]{2,1,3,0:T(8,128)S(1)}, u32[]{:S(2)}, u32[]{:S(2)}) collective-permute-start(f32[3,16,40,4]{2,1,3,0:T(8,128)S(1)} %copy.18), channel_id=1, source_target_pairs={{0,1},{1,2},{2,3},{3,4},{4,5},{5,6},{6,7},{7,0},{8,9},{9,10},{10,1... | collective-permute-start | bytes 92168 | tf_op jit(solution)/shard_map/ppermute | solution.py:25
  44.0 6.8 %collective-permute-start.5 = (f32[3,16,40,4]{2,1,3,0:T(8,128)S(1)}, f32[3,16,40,4]{2,1,3,0:T(8,128)S(1)}, u32[]{:S(2)}, u32[]{:S(2)}) collective-permute-start(f32[3,16,40,4]{2,1,3,0:T(8,128)S(1)} %copy.19), channel_id=1, source_target_pairs={{1,0},{2,1},{3,2},{4,3},{5,4},{6,5},{7,6},{0,7},{9,8},{10,9},{11,1... | collective-permute-start | bytes 92168 | tf_op jit(solution)/shard_map/ppermute | solution.py:28
  150.4 5.1 %copy-start.4 = (bf16[16,8,32,128]{3,2,1,0:T(8,128)(2,1)S(1)}, bf16[16,8,32,128]{3,2,1,0:T(8,128)(2,1)}, u32[]{:S(2)}) copy-start(bf16[16,8,32,128]{3,2,1,0:T(8,128)(2,1)} %param.10) | copy-start | bytes 3145732
where the time goes:
time: 157 us
  blocking collectives  62.4 us (40%)
  starting transfers between devices  36.7 us (23%)
  matrix products  19.1 us (12%)
  between operations  11.8 us (8%)
  other arithmetic  10.2 us (6%)
  waiting for transfers between devices  9.49 us (6%)
  local copies, waits for them, and re-layouts  7.06 us (4%)
    psum x5, blocking collectives, by_axis(): array = lax.psum(array, axis)  62.4 us
    ppermute x3, starting transfers between devices, extended(): lax.ppermute(lax.slice_in_dim(block, 0, width, axis=dim), axis, backward)  28.7 us
    ppermute x3, starting transfers between devices, extended(): lax.ppermute(lax.slice_in_dim(block, block.shape[dim] - width, None, axis...  8.02 us
    ppermute x3, waiting for transfers between devices, extended(): lax.ppermute(lax.slice_in_dim(block, block.shape[dim] - width, None, axis...  6.23 us
    sub x3, other arithmetic, chebyshev_next(): return 2.0 * scaled - earlier  3.83 us
    dot_general x5, matrix products, coordinates(): jnp.dot(gram_block, residue, precision=precise)  3.78 us
    another operation x2, local copies, waits for them, and re-layouts, body(): basis = jnp.stack(search_basis + residue_basis)  3.75 us
    ppermute x3, waiting for transfers between devices, extended(): lax.ppermute(lax.slice_in_dim(block, 0, width, axis=dim), axis, backward)  3.26 us
  transfers between devices with their start and end apart: 6, of which 5 were waited for; matrix products, arithmetic and copies ran while one was open for 1% of the time, Pallas kernels for 0%

commit v1 on v0

v1 whole, which is shorter than its diff:
```python
import jax
import jax.numpy as jnp
from jax import lax
from jax.experimental import pallas as pl
from jax.experimental.pallas import tpu as pltpu
from jax.sharding import PartitionSpec as P

S = 4
MESH = pl.DeviceIdType.MESH
LOW = 4
ROW = 16
DIR0, RES0, DIAG, DIR1, DIR2, DIR3, DIR4, RES1, RES2, RES3 = range(10)
BASIS = (DIR0, DIR1, DIR2, DIR3, DIR4, RES0, RES1, RES2, RES3)
NB = 9
NR = 16


def rolled(value, shift, axis):
    size = value.shape[axis]
    shift = shift % size
    return pltpu.roll(value, shift, axis) if shift else value


def kernel(
    dir_h, res_h, diag_h, rec_h, img_h, c_ref,
    out_update, out_residual, out_direction,
    fld, edge, rnd, rec_v, img_v,
    strip, strip_low, strip_high, merged,
    tile_send, tile_low, tile_high,
    sums, buf_zc, buf_y, buf_x,
    local_sem, send_sem, recv_sem, zc_send, zc_recv, y_send, y_recv, x_send, x_recv,
):
    nx, ny, nz = lax.axis_size("gx"), lax.axis_size("gy"), lax.axis_size("gz")
    half = nx // 2
    gx, gy, gz = lax.axis_index("gx"), lax.axis_index("gy"), lax.axis_index("gz")
    col = lax.rem(gx, half)
    block = gx - col
    me_zc = lax.div(gx, half) * ny + gy
    x_up = (lax.rem(gx + 1, nx), gy, gz)
    x_down = (lax.rem(gx + nx - 1, nx), gy, gz)
    y_up = (gx, lax.rem(gy + 1, ny), gz)
    y_down = (gx, lax.rem(gy + ny - 1, ny), gz)
    z_up = (gx, gy, lax.rem(gz + 1, nz))
    z_down = (gx, gy, lax.rem(gz + nz - 1, nz))

    def zc_peer(offset):
        peer = lax.rem(me_zc + offset, 2 * ny)
        return peer, (lax.div(peer, ny) * half + col, lax.rem(peer, ny), gz)

    def y_peer(offset):
        peer = lax.rem(col + offset, half)
        return peer, (block + peer, gy, gz)

    def x_peer(offset):
        peer = lax.rem(gz + offset, nz)
        return peer, (gx, gy, peer)

    sources = (dir_h, res_h, diag_h)
    locals_ = []
    for i, src in enumerate(sources):
        locals_.append(pltpu.make_async_copy(src, fld.at[i, LOW:LOW + 8, ROW:ROW + 32], local_sem.at[i]))
    locals_.append(pltpu.make_async_copy(img_h, img_v, local_sem.at[3]))
    locals_.append(pltpu.make_async_copy(rec_h, rec_v, local_sem.at[4]))
    for copy in locals_:
        copy.start()

    barrier = pltpu.get_barrier_semaphore()
    greeted = [x_up, x_down, y_up, y_down, z_up, z_down]
    greeted += [zc_peer(o)[1] for o in range(1, 2 * ny)]
    greeted += [y_peer(o)[1] for o in range(1, half)]
    greeted += [x_peer(o)[1] for o in range(1, nz)]
    for device in greeted:
        pl.semaphore_signal(barrier, inc=1, device_id=device, device_id_type=MESH)
    pl.semaphore_wait(barrier, len(greeted))

    used = [0]

    def send(src, dst, device):
        i = used[0]
        used[0] += 1
        copy = pltpu.make_async_remote_copy(
            src_ref=src, dst_ref=dst, send_sem=send_sem.at[i], recv_sem=recv_sem.at[i],
            device_id=device, device_id_type=MESH,
        )
        copy.start()
        return copy

    x_copies = []
    for i, (src, depth) in enumerate(zip(sources, (4, 3, 3))):
        x_copies.append(send(src.at[8 - depth:8], fld.at[i, LOW - depth:LOW, ROW:ROW + 32], x_up))
        x_copies.append(send(src.at[0:depth], fld.at[i, LOW + 8:LOW + 8 + depth, ROW:ROW + 32], x_down))
    y_copies = []
    for i, src in enumerate(sources):
        y_copies.append(send(src.at[:, 24:32], fld.at[i, LOW:LOW + 8, ROW - 8:ROW], y_up))
        y_copies.append(send(src.at[:, 0:8], fld.at[i, LOW:LOW + 8, ROW + 32:ROW + 40], y_down))

    for copy in locals_[:3]:
        copy.wait()

    lane8 = lax.broadcasted_iota(jnp.int32, (8, 128), 1)
    group8 = lane8 // 8

    @pl.loop(0, 6)
    def _(n):
        i, h = n // 2, n % 2
        packed = jnp.zeros((8, 128), jnp.float32)
        for q in range(16):
            t, x = q // 4, q % 4
            tile = fld[i, LOW + 4 * h + x, ROW + 8 * t:ROW + 8 * t + 8, :]
            packed = jnp.where(group8 == q, rolled(tile, 4 + 8 * q, 1), packed)
        strip[i, h] = packed

    z_copies = [send(strip, strip_low, z_up), send(strip, strip_high, z_down)]
    for copy in z_copies:
        copy.wait()
    from_low = lane8 % 8 < 4
    for i in range(3):
        for h in range(2):
            merged[i, 1 + h] = jnp.where(from_low, strip_low[i, h], strip_high[i, h])
    x_copies.append(send(merged.at[:, 2], merged.at[:, 0], x_up))
    x_copies.append(send(merged.at[:, 1], merged.at[:, 3], x_down))
    for copy in x_copies:
        copy.wait()

    for i, depth in ((0, 3), (1, 2), (2, 2)):
        for first in (LOW - depth, LOW + 8):
            layers = slice(first, first + depth)
            y_copies.append(send(fld.at[i, layers, ROW + 24:ROW + 32], fld.at[i, layers, ROW - 8:ROW], y_up))
            y_copies.append(send(fld.at[i, layers, ROW:ROW + 8], fld.at[i, layers, ROW + 32:ROW + 40], y_down))
    for i in range(3):
        last = jnp.zeros((8, 128), jnp.float32)
        first = jnp.zeros((8, 128), jnp.float32)
        for b in range(4):
            here = (lane8 // 32) == b
            value = merged[i, b]
            last = jnp.where(here, rolled(value, 32 * b - 96, 1), last)
            first = jnp.where(here, rolled(value, 32 * b, 1), first)
        tile_send[0, i] = last
        tile_send[1, i] = first
    y_copies.append(send(tile_send.at[0], tile_low, y_up))
    y_copies.append(send(tile_send.at[1], tile_high, y_down))

    for i in range(3):
        @pl.loop(0, 4)
        def _(b):
            value = merged[i, b]
            for q in range(16):
                t, x = q // 4, q % 4
                edge[i, 4 * b + x, ROW + 8 * t:ROW + 8 * t + 8, :] = rolled(value, -8 * q - 4, 1)

    for copy in y_copies:
        copy.wait()
    for i in range(3):
        low, high = tile_low[i], tile_high[i]
        for x in range(16):
            edge[i, x, ROW - 8:ROW, :] = rolled(low, -8 * x - 4, 1)
            edge[i, x, ROW + 32:ROW + 40, :] = rolled(high, -8 * x - 4, 1)

    def apply(mine, other, into, current, earlier, first, last, top, bottom):
        lane = lax.broadcasted_iota(jnp.int32, (bottom - top, 128), 1)

        @pl.loop(first, last)
        def _(x):
            centre = mine[current, x, top:bottom, :]
            beside = other[current, x, top:bottom, :]
            total = mine[current, x + 1, top:bottom, :] + mine[current, x - 1, top:bottom, :]
            total = total + mine[current, x, top + 1:bottom + 1, :] + mine[current, x, top - 1:bottom - 1, :]
            total = total + pltpu.roll(jnp.where(lane == 0, beside, centre), 127, 1)
            total = total + pltpu.roll(jnp.where(lane == 127, beside, centre), 1, 1)
            result = (mine[DIAG, x, top:bottom, :] - 1.25) * centre - total
            if earlier is None:
                result = result * (1.0 / 6.75)
            else:
                result = result * (2.0 / 6.75) - mine[earlier, x, top:bottom, :]
            mine[into, x, top:bottom, :] = result

    def advance(into, current, earlier, reach):
        if reach == 0:
            apply(fld, edge, into, current, earlier, LOW, LOW + 8, ROW, ROW + 32)
            return
        apply(fld, edge, into, current, earlier, LOW - reach, LOW + 8 + reach, ROW - 8, ROW + 40)
        wide = reach - 1
        apply(edge, fld, into, current, earlier, LOW - wide, LOW + 8 + wide, ROW - 8, ROW + 40)

    advance(DIR1, DIR0, None, 3)
    advance(RES1, RES0, None, 2)
    advance(DIR2, DIR1, DIR0, 2)
    advance(RES2, RES1, RES0, 1)
    advance(DIR3, DIR2, DIR1, 1)
    advance(RES3, RES2, RES1, 0)
    advance(DIR4, DIR3, DIR2, 0)

    pairs = [(i, j) for i in range(NB) for j in range(i, NB)]
    zero = jnp.zeros((8, 128), jnp.float32)

    def gram_step(n, totals):
        x, row = n // 4, pl.multiple_of((n % 4) * 8, 8)
        values = [fld[p, LOW + x, pl.ds(ROW + row, 8), :] for p in BASIS]
        for j, value in enumerate(values):
            rnd[j, x, pl.ds(row, 8), :] = value.astype(jnp.bfloat16).astype(jnp.float32)
        return tuple(t + values[i] * values[j] for t, (i, j) in zip(totals, pairs))

    totals = lax.fori_loop(0, 32, gram_step, (zero,) * len(pairs))
    sums[...] = jnp.zeros_like(sums)
    for total, (i, j) in zip(totals, pairs):
        row = jnp.sum(total, axis=0, keepdims=True)
        sums[9 * i + j:9 * i + j + 1, :] = row
        if i != j:
            sums[9 * j + i:9 * j + i + 1, :] = row

    locals_[3].wait()

    @pl.loop(0, NR // 2)
    def _(pair):
        def projection_step(n, totals):
            x, row = n // 2, pl.multiple_of((n % 2) * 16, 16)
            images = [img_v[2 * pair + m, x, pl.ds(row, 16), :].astype(jnp.float32) for m in range(2)]
            result = []
            for j in range(NB):
                value = rnd[j, x, pl.ds(row, 16), :]
                for m in range(2):
                    product = images[m] * value
                    result.append(totals[2 * j + m] + (product[:8] + product[8:]))
            return tuple(result)

        totals = lax.fori_loop(0, 16, projection_step, (zero,) * (2 * NB))
        for j in range(NB):
            for m in range(2):
                sums[pl.ds(128 + 16 * j + 2 * pair + m, 1), :] = jnp.sum(totals[2 * j + m], axis=0, keepdims=True)

    packed = lax.dot_general(
        jnp.ones((8, 128), jnp.float32), sums[...], (((1,), (1,)), ((), ())),
        precision=lax.Precision.HIGHEST, preferred_element_type=jnp.float32,
    )
    own = jnp.concatenate([packed[0:1, 128 * g:128 * g + 128] for g in range(4)], axis=0)

    def exchange(value, buf, me, peers, count, sends, recvs):
        buf[pl.ds(me, 1)] = value[None]
        copies = []
        for o in range(1, count):
            _, device = peers(o)
            copy = pltpu.make_async_remote_copy(
                src_ref=buf.at[me], dst_ref=buf.at[me], send_sem=sends.at[o], recv_sem=recvs.at[me],
                device_id=device, device_id_type=MESH,
            )
            copy.start()
            copies.append(copy)
        for o in range(1, count):
            peer, device = peers(o)
            pltpu.make_async_remote_copy(
                src_ref=buf.at[peer], dst_ref=buf.at[peer], send_sem=sends.at[o], recv_sem=recvs.at[peer],
                device_id=device, device_id_type=MESH,
            ).wait_recv()
        for copy in copies:
            copy.wait_send()
        return jnp.sum(buf[...], axis=0)

    own = exchange(own, buf_zc, me_zc, zc_peer, 2 * ny, zc_send, zc_recv)
    own = exchange(own, buf_y, col, y_peer, half, y_send, y_recv)
    own = exchange(own, buf_x, gz, x_peer, nz, x_send, x_recv)

    shape = (16, 128)
    sub = lax.broadcasted_iota(jnp.int32, shape, 0)
    lane = lax.broadcasted_iota(jnp.int32, shape, 1)
    gram = jnp.zeros(shape, jnp.float32)
    for i in range(NB):
        gram = jnp.where(sub == i, jnp.broadcast_to(rolled(own[0:1], -9 * i, 1), shape), gram)
    gram = jnp.where(lane < NB, gram, 0.0)
    proj = jnp.zeros(shape, jnp.float32)
    for j in range(NB):
        proj = jnp.where(sub == j, jnp.broadcast_to(rolled(own[1 + j // 8:2 + j // 8], -16 * j, 1), shape), proj)

    def recurrence(index):
        def among(*which):
            hit = index == which[0]
            for w in which[1:]:
                hit = jnp.logical_or(hit, index == w)
            return hit
        before = jnp.where(among(1, 6), 6.75, jnp.where(among(2, 3, 4, 7, 8), 3.375, 0.0))
        at = jnp.where(among(0, 1, 2, 3, 5, 6, 7), 7.25, 0.0)
        after = jnp.where(among(0, 1, 2, 5, 6), 3.375, 0.0)
        return before, at, after

    coeffs = (recurrence(sub), recurrence(lane))

    def mapped_of(vector, axis):
        before, at, after = coeffs[axis]
        return before * rolled(vector, 1, axis) + at * vector + after * rolled(vector, -1, axis)

    def form(left, right):
        return jnp.broadcast_to(jnp.sum(jnp.sum(gram * left * right, axis=1, keepdims=True), axis=0, keepdims=True), shape)

    residue = [jnp.where(k == S + 1, 1.0, 0.0) for k in (sub, lane)]
    search = [jnp.where(k == 0, 1.0, 0.0) for k in (sub, lane)]
    update = jnp.zeros(shape, jnp.float32)
    norm_now = form(residue[0], residue[1])
    for _ in range(S):
        mapped = [mapped_of(search[a], a) for a in range(2)]
        step = norm_now / form(search[0], mapped[1])
        update = update + step * search[0]
        residue = [residue[a] - step * mapped[a] for a in range(2)]
        norm_next = form(residue[0], residue[1])
        ratio = norm_next / norm_now
        search = [residue[a] + ratio * search[a] for a in range(2)]
        norm_now = norm_next
    inner = jnp.sum(proj * residue[0], axis=0, keepdims=True)
    weights = jnp.sum(c_ref[...] * inner[:, :NR], axis=1, keepdims=True)
    weights = jnp.broadcast_to(weights.astype(jnp.bfloat16).astype(jnp.float32), (NR, 128))

    locals_[4].wait()

    def spread(vector, i):
        return jnp.broadcast_to(vector[i:i + 1, :], (8, 128))

    ups = [spread(update, i) for i in range(NB)]
    ress = [spread(residue[0], i) for i in range(NB)]
    seas = [spread(search[0], i) for i in range(NB)]

    @pl.loop(0, 32)
    def _(n):
        x, row = n // 4, pl.multiple_of((n % 4) * 8, 8)
        u = r = s = None
        for i, p in enumerate(BASIS):
            value = fld[p, LOW + x, pl.ds(ROW + row, 8), :]
            u = ups[i] * value if u is None else u + ups[i] * value
            r = ress[i] * value if r is None else r + ress[i] * value
            s = seas[i] * value if s is None else s + seas[i] * value
        out_update[x, pl.ds(row, 8), :] = u
        out_residual[x, pl.ds(row, 8), :] = r
        out_direction[x, pl.ds(row, 8), :] = s

    ws = [jnp.broadcast_to(weights[k:k + 1, :], (16, 128)) for k in range(NR)]

    @pl.loop(0, 16)
    def _(n):
        x, row = n // 2, pl.multiple_of((n % 2) * 16, 16)
        total = None
        for k in range(NR):
            term = ws[k] * rec_v[k, x, pl.ds(row, 16), :].astype(jnp.float32)
            total = term if total is None else total + term
        out_direction[x, pl.ds(row, 16), :] = out_direction[x, pl.ds(row, 16), :] - total


def body(residual, direction, diagonal, recycled, recycled_images, coupling_inverse):
    f32 = jnp.float32
    ny, nz = lax.axis_size("gy"), lax.axis_size("gz")
    half = lax.axis_size("gx") // 2
    anywhere = pl.BlockSpec(memory_space=pl.ANY)
    vmem = pl.BlockSpec(memory_space=pltpu.VMEM)
    tile = (8, 128)
    copies = 48
    return pl.pallas_call(
        kernel,
        out_shape=[jax.ShapeDtypeStruct(residual.shape, f32)] * 3,
        in_specs=[anywhere] * 5 + [vmem],
        out_specs=[vmem] * 3,
        scratch_shapes=[
            pltpu.VMEM((10, 16, 64, 128), f32),
            pltpu.VMEM((10, 16, 64, 128), f32),
            pltpu.VMEM((NB, 8, 32, 128), f32),
            pltpu.VMEM(recycled.shape, jnp.bfloat16),
            pltpu.VMEM(recycled.shape, jnp.bfloat16),
            pltpu.VMEM((3, 2) + tile, f32),
            pltpu.VMEM((3, 2) + tile, f32),
            pltpu.VMEM((3, 2) + tile, f32),
            pltpu.VMEM((3, 4) + tile, f32),
            pltpu.VMEM((2, 3) + tile, f32),
            pltpu.VMEM((3,) + tile, f32),
            pltpu.VMEM((3,) + tile, f32),
            pltpu.VMEM((512, 128), f32),
            pltpu.VMEM((2 * ny, 4, 128), f32),
            pltpu.VMEM((half, 4, 128), f32),
            pltpu.VMEM((nz, 4, 128), f32),
            pltpu.SemaphoreType.DMA((5,)),
            pltpu.SemaphoreType.DMA((copies,)),
            pltpu.SemaphoreType.DMA((copies,)),
            pltpu.SemaphoreType.DMA((2 * ny,)),
            pltpu.SemaphoreType.DMA((2 * ny,)),
            pltpu.SemaphoreType.DMA((half,)),
            pltpu.SemaphoreType.DMA((half,)),
            pltpu.SemaphoreType.DMA((nz,)),
            pltpu.SemaphoreType.DMA((nz,)),
        ],
        compiler_params=pltpu.CompilerParams(collective_id=0, has_side_effects=True),
        name="block",
    )(direction, residual, diagonal, recycled, recycled_images, coupling_inverse)


def solution(mesh):
    field = P("gx", "gy", "gz")
    many = P(None, "gx", "gy", "gz")
    return jax.shard_map(
        body, mesh=mesh,
        in_specs=(field, field, field, many, many, P()),
        out_specs=(field, field, field),
        check_vma=False,
    )
```

time: 157 us -> 73.9 us (0.47)
  the two profiles are of different devices: /device:TPU:8 before, /device:TPU:16 now
where the time goes in v1:
time: 73.9 us; the launch traced here: 73.6 us
  Pallas kernels  69.8 us (94%)
  local copies, waits for them, and re-layouts  3.21 us (4%)
    pallas_call x1, Pallas kernels, body(): pl.pallas_call(kernel, out_shape=[jax.ShapeDtypeStruct(residual.shape, f3...  69.8 us
    unnamed x7, local copies, waits for them, and re-layouts  3.21 us

profile of v1, /device:TPU:16, one launch (start us, length us, event | category | flops | bytes accessed | tf_op | source)
XLA Modules:
  0.0 73.6 jit_solution(18256798137985127626)
XLA Ops:
  0.6 69.8 %block.1 = (f32[8,32,128]{2,1,0:T(8,128)}, f32[8,32,128]{2,1,0:T(8,128)}, f32[8,32,128]{2,1,0:T(8,128)}) custom-call(f32[8,32,128]{2,1,0:T(8,128)} %dir_h.1, f32[8,32,128]{2,1,0:T(8,128)} %res_h.1, f32[8,32,128]{2,1,0:T(8,128)} %diag_h.1, bf16[16,8,32,128]{3,2,1,0:T(8,128)(2,1)} %rec_h.1, bf16[16,8,32,128]{3,2,1,0:T(8,128)(2,1)} %img_h.1, f32[16,16]{1,0:T(8,128)} %c_ref.1), custom_call_target="tpu_custom_call" | custom-call | tf_op jit(solution)/shard_map/block/pallas_call | solution.py:352
  70.4 0.0 copy-start.1
  70.4 1.6 %copy.12 = f32[8,32,128]{2,1,0:T(8,128)} copy(f32[8,32,128]{2,1,0:T(8,128)} %get-tuple-element.6) | data formatting | bytes 262144
  72.0 0.0 copy-done.1
  72.0 0.0 copy-start
  72.0 0.7 copy.13
  72.7 0.3 copy-done
  73.0 0.7 copy.14
Async XLA Ops:
  70.4 1.6 %copy-start.1 = (f32[8,32,128]{2,1,0:T(8,128)S(1)}, f32[8,32,128]{2,1,0:T(8,128)}, u32[]{:S(2)}) copy-start(f32[8,32,128]{2,1,0:T(8,128)} %get-tuple-element.7) | copy-start | bytes 393220
  72.0 1.0 %copy-start = (f32[8,32,128]{2,1,0:T(8,128)S(1)}, f32[8,32,128]{2,1,0:T(8,128)}, u32[]{:S(2)}) copy-start(f32[8,32,128]{2,1,0:T(8,128)} %get-tuple-element.8) | copy-start | bytes 393220

commit v2 on v1

--- a/solution.py
+++ b/solution.py
@@ -22,13 +22,13 @@
 
 
 def kernel(
-    dir_h, res_h, diag_h, rec_h, img_h, c_ref,
-    out_update, out_residual, out_direction,
-    fld, edge, rnd, rec_v, img_v,
+    dir_h, res_h, diag_h, img_h, c_ref,
+    basis_out, coord_out,
+    fld, edge, rnd, img_v,
     strip, strip_low, strip_high, merged,
     tile_send, tile_low, tile_high,
     sums, buf_zc, buf_y, buf_x,
-    local_sem, send_sem, recv_sem, zc_send, zc_recv, y_send, y_recv, x_send, x_recv,
+    local_sem, out_sem, send_sem, recv_sem, zc_send, zc_recv, y_send, y_recv, x_send, x_recv,
 ):
     nx, ny, nz = lax.axis_size("gx"), lax.axis_size("gy"), lax.axis_size("gz")
     half = nx // 2
@@ -60,7 +60,6 @@
     for i, src in enumerate(sources):
         locals_.append(pltpu.make_async_copy(src, fld.at[i, LOW:LOW + 8, ROW:ROW + 32], local_sem.at[i]))
     locals_.append(pltpu.make_async_copy(img_h, img_v, local_sem.at[3]))
-    locals_.append(pltpu.make_async_copy(rec_h, rec_v, local_sem.at[4]))
     for copy in locals_:
         copy.start()
 
@@ -100,15 +99,14 @@
     lane8 = lax.broadcasted_iota(jnp.int32, (8, 128), 1)
     group8 = lane8 // 8
 
-    @pl.loop(0, 6)
-    def _(n):
-        i, h = n // 2, n % 2
-        packed = jnp.zeros((8, 128), jnp.float32)
-        for q in range(16):
-            t, x = q // 4, q % 4
-            tile = fld[i, LOW + 4 * h + x, ROW + 8 * t:ROW + 8 * t + 8, :]
-            packed = jnp.where(group8 == q, rolled(tile, 4 + 8 * q, 1), packed)
-        strip[i, h] = packed
+    for i in range(3):
+        for h in range(2):
+            packed = jnp.zeros((8, 128), jnp.float32)
+            for q in range(16):
+                t, x = q // 4, q % 4
+                tile = fld[i, LOW + 4 * h + x, ROW + 8 * t:ROW + 8 * t + 8, :]
+                packed = jnp.where(group8 == q, rolled(tile, 4 + 8 * q, 1), packed)
+            strip[i, h] = packed
 
     z_copies = [send(strip, strip_low, z_up), send(strip, strip_high, z_down)]
     for copy in z_copies:
@@ -119,6 +117,16 @@
             merged[i, 1 + h] = jnp.where(from_low, strip_low[i, h], strip_high[i, h])
     x_copies.append(send(merged.at[:, 2], merged.at[:, 0], x_up))
     x_copies.append(send(merged.at[:, 1], merged.at[:, 3], x_down))
+
+    def place(b):
+        for i in range(3):
+            value = merged[i, b]
+            for q in range(16):
+                t, x = q // 4, q % 4
+                edge[i, 4 * b + x, ROW + 8 * t:ROW + 8 * t + 8, :] = rolled(value, -8 * q - 4, 1)
+
+    place(1)
+    place(2)
     for copy in x_copies:
         copy.wait()
 
@@ -140,14 +148,8 @@
     y_copies.append(send(tile_send.at[0], tile_low, y_up))
     y_copies.append(send(tile_send.at[1], tile_high, y_down))
 
-    for i in range(3):
-        @pl.loop(0, 4)
-        def _(b):
-            value = merged[i, b]
-            for q in range(16):
-                t, x = q // 4, q % 4
-                edge[i, 4 * b + x, ROW + 8 * t:ROW + 8 * t + 8, :] = rolled(value, -8 * q - 4, 1)
-
+    place(0)
+    place(3)
     for copy in y_copies:
         copy.wait()
     for i in range(3):
@@ -159,8 +161,7 @@
     def apply(mine, other, into, current, earlier, first, last, top, bottom):
         lane = lax.broadcasted_iota(jnp.int32, (bottom - top, 128), 1)
 
-        @pl.loop(first, last)
-        def _(x):
+        for x in range(first, last):
             centre = mine[current, x, top:bottom, :]
             beside = other[current, x, top:bottom, :]
             total = mine[current, x + 1, top:bottom, :] + mine[current, x - 1, top:bottom, :]
@@ -182,6 +183,16 @@
         wide = reach - 1
         apply(edge, fld, into, current, earlier, LOW - wide, LOW + 8 + wide, ROW - 8, ROW + 40)
 
+    basis_copies = []
+
+    def put_out(plane):
+        j = BASIS.index(plane)
+        copy = pltpu.make_async_copy(fld.at[plane, LOW:LOW + 8, ROW:ROW + 32], basis_out.at[j], out_sem.at[j])
+        copy.start()
+        basis_copies.append(copy)
+
+    put_out(DIR0)
+    put_out(RES0)
     advance(DIR1, DIR0, None, 3)
     advance(RES1, RES0, None, 2)
     advance(DIR2, DIR1, DIR0, 2)
@@ -190,40 +201,52 @@
     advance(RES3, RES2, RES1, 0)
     advance(DIR4, DIR3, DIR2, 0)
 
-    pairs = [(i, j) for i in range(NB) for j in range(i, NB)]
+    for plane in (DIR1, RES1, DIR2, RES2, DIR3, RES3, DIR4):
+        put_out(plane)
+
+    sums[...] = jnp.zeros_like(sums)
     zero = jnp.zeros((8, 128), jnp.float32)
 
-    def gram_step(n, totals):
-        x, row = n // 4, pl.multiple_of((n % 4) * 8, 8)
-        values = [fld[p, LOW + x, pl.ds(ROW + row, 8), :] for p in BASIS]
-        for j, value in enumerate(values):
-            rnd[j, x, pl.ds(row, 8), :] = value.astype(jnp.bfloat16).astype(jnp.float32)
-        return tuple(t + values[i] * values[j] for t, (i, j) in zip(totals, pairs))
-
-    totals = lax.fori_loop(0, 32, gram_step, (zero,) * len(pairs))
-    sums[...] = jnp.zeros_like(sums)
-    for total, (i, j) in zip(totals, pairs):
-        row = jnp.sum(total, axis=0, keepdims=True)
-        sums[9 * i + j:9 * i + j + 1, :] = row
-        if i != j:
-            sums[9 * j + i:9 * j + i + 1, :] = row
+    def gram_pass(pairs, store):
+        first = pairs[0][0]
+
+        def step(x, totals):
+            for t in range(4):
+                rows = slice(8 * t, 8 * t + 8)
+                values = {j: fld[BASIS[j], LOW + x, ROW + 8 * t:ROW + 8 * t + 8, :] for j in range(first, NB)}
+                if store:
+                    for j, value in values.items():
+                        rnd[j, x, rows, :] = value.astype(jnp.bfloat16).astype(jnp.float32)
+                totals = [total + values[i] * values[j] for total, (i, j) in zip(totals, pairs)]
+            return tuple(totals)
+
+        totals = lax.fori_loop(0, 8, step, (zero,) * len(pairs))
+        for total, (i, j) in zip(totals, pairs):
+            row = jnp.sum(total, axis=0, keepdims=True)
+            sums[9 * i + j:9 * i + j + 1, :] = row
+            if i != j:
+                sums[9 * j + i:9 * j + i + 1, :] = row
+
+    gram_pass([(i, j) for i in range(3) for j in range(i, NB)], True)
+    gram_pass([(i, j) for i in range(3, NB) for j in range(i, NB)], False)
 
     locals_[3].wait()
 
     @pl.loop(0, NR // 2)
     def _(pair):
         def projection_step(n, totals):
-            x, row = n // 2, pl.multiple_of((n % 2) * 16, 16)
-            images = [img_v[2 * pair + m, x, pl.ds(row, 16), :].astype(jnp.float32) for m in range(2)]
-            result = []
-            for j in range(NB):
-                value = rnd[j, x, pl.ds(row, 16), :]
-                for m in range(2):
-                    product = images[m] * value
-                    result.append(totals[2 * j + m] + (product[:8] + product[8:]))
-            return tuple(result)
-
-        totals = lax.fori_loop(0, 16, projection_step, (zero,) * (2 * NB))
+            totals = list(totals)
+            for k in range(4):
+                x, row = 2 * n + k // 2, 16 * (k % 2)
+                images = [img_v[2 * pair + m, x, row:row + 16, :].astype(jnp.float32) for m in range(2)]
+                for j in range(NB):
+                    value = rnd[j, x, row:row + 16, :]
+                    for m in range(2):
+                        product = images[m] * value
+                        totals[2 * j + m] = totals[2 * j + m] + (product[:8] + product[8:])
+            return tuple(totals)
+
+        totals = lax.fori_loop(0, 4, projection_step, (zero,) * (2 * NB))
         for j in range(NB):
             for m in range(2):
                 sums[pl.ds(128 + 16 * j + 2 * pair + m, 1), :] = jnp.sum(totals[2 * j + m], axis=0, keepdims=True)
@@ -270,75 +293,75 @@
     for j in range(NB):
         proj = jnp.where(sub == j, jnp.broadcast_to(rolled(own[1 + j // 8:2 + j // 8], -16 * j, 1), shape), proj)
 
-    def recurrence(index):
-        def among(*which):
-            hit = index == which[0]
-            for w in which[1:]:
-                hit = jnp.logical_or(hit, index == w)
-            return hit
-        before = jnp.where(among(1, 6), 6.75, jnp.where(among(2, 3, 4, 7, 8), 3.375, 0.0))
-        at = jnp.where(among(0, 1, 2, 3, 5, 6, 7), 7.25, 0.0)
-        after = jnp.where(among(0, 1, 2, 5, 6), 3.375, 0.0)
-        return before, at, after
-
-    coeffs = (recurrence(sub), recurrence(lane))
-
-    def mapped_of(vector, axis):
-        before, at, after = coeffs[axis]
-        return before * rolled(vector, 1, axis) + at * vector + after * rolled(vector, -1, axis)
-
-    def form(left, right):
-        return jnp.broadcast_to(jnp.sum(jnp.sum(gram * left * right, axis=1, keepdims=True), axis=0, keepdims=True), shape)
-
-    residue = [jnp.where(k == S + 1, 1.0, 0.0) for k in (sub, lane)]
-    search = [jnp.where(k == 0, 1.0, 0.0) for k in (sub, lane)]
+    def among(*which):
+        hit = sub == which[0]
+        for w in which[1:]:
+            hit = jnp.logical_or(hit, sub == w)
+        return hit
+
+    before = jnp.where(among(1, 6), 6.75, jnp.where(among(2, 3, 4, 7, 8), 3.375, 0.0))
+    at = jnp.where(among(0, 1, 2, 3, 5, 6, 7), 7.25, 0.0)
+    after = jnp.where(among(0, 1, 2, 5, 6), 3.375, 0.0)
+
+    def mapped_of(vector):
+        return before * rolled(vector, 1, 0) + at * vector + after * rolled(vector, -1, 0)
+
+    def along_rows(value):
+        return jnp.broadcast_to(jnp.sum(value, axis=0, keepdims=True), shape)
+
+    def along_lanes(value):
+        return jnp.broadcast_to(jnp.sum(value, axis=1, keepdims=True), shape)
+
+    residue = jnp.where(sub == S + 1, 1.0, 0.0)
+    search = jnp.where(sub == 0, 1.0, 0.0)
     update = jnp.zeros(shape, jnp.float32)
-    norm_now = form(residue[0], residue[1])
+    gram_residue = along_lanes(jnp.where(lane == S + 1, gram, 0.0))
+    norm_now = along_rows(residue * gram_residue)
     for _ in range(S):
-        mapped = [mapped_of(search[a], a) for a in range(2)]
-        step = norm_now / form(search[0], mapped[1])
-        update = update + step * search[0]
-        residue = [residue[a] - step * mapped[a] for a in range(2)]
-        norm_next = form(residue[0], residue[1])
-        ratio = norm_next / norm_now
-        search = [residue[a] + ratio * search[a] for a in range(2)]
+        mapped = mapped_of(search)
+        gram_mapped = along_lanes(gram * along_rows(jnp.where(sub == lane, mapped, 0.0)))
+        step = norm_now / along_rows(search * gram_mapped)
+        update = update + step * search
+        residue = residue - step * mapped
+        gram_residue = gram_residue - step * gram_mapped
+        norm_next = along_rows(residue * gram_residue)
+        search = residue + (norm_next / norm_now) * search
         norm_now = norm_next
-    inner = jnp.sum(proj * residue[0], axis=0, keepdims=True)
+    inner = jnp.sum(proj * residue, axis=0, keepdims=True)
     weights = jnp.sum(c_ref[...] * inner[:, :NR], axis=1, keepdims=True)
     weights = jnp.broadcast_to(weights.astype(jnp.bfloat16).astype(jnp.float32), (NR, 128))
-
-    locals_[4].wait()
-
-    def spread(vector, i):
-        return jnp.broadcast_to(vector[i:i + 1, :], (8, 128))
-
-    ups = [spread(update, i) for i in range(NB)]
-    ress = [spread(residue[0], i) for i in range(NB)]
-    seas = [spread(search[0], i) for i in range(NB)]
-
-    @pl.loop(0, 32)
-    def _(n):
-        x, row = n // 4, pl.multiple_of((n % 4) * 8, 8)
-        u = r = s = None
-        for i, p in enumerate(BASIS):
-            value = fld[p, LOW + x, pl.ds(ROW + row, 8), :]
-            u = ups[i] * value if u is None else u + ups[i] * value
-            r = ress[i] * value if r is None else r + ress[i] * value
-            s = seas[i] * value if s is None else s + seas[i] * value
-        out_update[x, pl.ds(row, 8), :] = u
-        out_residual[x, pl.ds(row, 8), :] = r
-        out_direction[x, pl.ds(row, 8), :] = s
-
-    ws = [jnp.broadcast_to(weights[k:k + 1, :], (16, 128)) for k in range(NR)]
-
-    @pl.loop(0, 16)
-    def _(n):
-        x, row = n // 2, pl.multiple_of((n % 2) * 16, 16)
-        total = None
-        for k in range(NR):
-            term = ws[k] * rec_v[k, x, pl.ds(row, 16), :].astype(jnp.float32)
-            total = term if total is None else total + term
-        out_direction[x, pl.ds(row, 16), :] = out_direction[x, pl.ds(row, 16), :] - total
+    for n, vector in enumerate((update, residue, search, weights)):
+        coord_out[16 * n:16 * n + 16, :] = vector
+    for copy in basis_copies:
+        copy.wait()
+
+
+def combine(basis, rec, coord, out_update, out_residual, out_direction):
+    def spread(n, i):
+        return jnp.broadcast_to(coord[16 * n + i:16 * n + i + 1, :], (8, 128))
+
+    factors = [[spread(n, i) for i in range(NB)] for n in range(3)]
+    for x in range(8):
+        for t in range(4):
+            rows = slice(8 * t, 8 * t + 8)
+            totals = [None] * 3
+            for i in range(NB):
+                value = basis[i, x, rows, :]
+                for n in range(3):
+                    term = factors[n][i] * value
+                    totals[n] = term if i == 0 else totals[n] + term
+            out_update[x, rows, :] = totals[0]
+            out_residual[x, rows, :] = totals[1]
+            out_direction[x, rows, :] = totals[2]
+    weights = [jnp.broadcast_to(coord[48 + k:49 + k, :], (16, 128)) for k in range(NR)]
+    for x in range(8):
+        for t in range(2):
+            rows = slice(16 * t, 16 * t + 16)
+            total = None
+            for k in range(NR):
+                term = weights[k] * rec[k, x, rows, :].astype(jnp.float32)
+                total = term if k == 0 else total + term
+            out_direction[x, rows, :] = out_direction[x, rows, :] - total
 
 
 def body(residual, direction, diagonal, recycled, recycled_images, coupling_inverse):
@@ -349,16 +372,19 @@
     vmem = pl.BlockSpec(memory_space=pltpu.VMEM)
     tile = (8, 128)
     copies = 48
-    return pl.pallas_call(
+    operands = [
+        pltpu.with_memory_space_constraint(x, pltpu.MemorySpace.HBM)
+        for x in (direction, residual, diagonal, recycled_images, coupling_inverse)
+    ]
+    basis, coord = pl.pallas_call(
         kernel,
-        out_shape=[jax.ShapeDtypeStruct(residual.shape, f32)] * 3,
-        in_specs=[anywhere] * 5 + [vmem],
-        out_specs=[vmem] * 3,
+        out_shape=[jax.ShapeDtypeStruct((NB,) + residual.shape, f32), jax.ShapeDtypeStruct((64, 128), f32)],
+        in_specs=[anywhere] * 4 + [vmem],
+        out_specs=[anywhere, vmem],
         scratch_shapes=[
             pltpu.VMEM((10, 16, 64, 128), f32),
             pltpu.VMEM((10, 16, 64, 128), f32),
             pltpu.VMEM((NB, 8, 32, 128), f32),
-            pltpu.VMEM(recycled.shape, jnp.bfloat16),
             pltpu.VMEM(recycled.shape, jnp.bfloat16),
             pltpu.VMEM((3, 2) + tile, f32),
             pltpu.VMEM((3, 2) + tile, f32),
@@ -371,7 +397,8 @@
             pltpu.VMEM((2 * ny, 4, 128), f32),
             pltpu.VMEM((half, 4, 128), f32),
             pltpu.VMEM((nz, 4, 128), f32),
-            pltpu.SemaphoreType.DMA((5,)),
+            pltpu.SemaphoreType.DMA((4,)),
+            pltpu.SemaphoreType.DMA((NB,)),
             pltpu.SemaphoreType.DMA((copies,)),
             pltpu.SemaphoreType.DMA((copies,)),
             pltpu.SemaphoreType.DMA((2 * ny,)),
@@ -381,9 +408,17 @@
             pltpu.SemaphoreType.DMA((nz,)),
             pltpu.SemaphoreType.DMA((nz,)),
         ],
-        compiler_params=pltpu.CompilerParams(collective_id=0, has_side_effects=True),
+        compiler_params=pltpu.CompilerParams(collective_id=0, has_side_effects=True, vmem_limit_bytes=24 * 2**20),
         name="block",
-    )(direction, residual, diagonal, recycled, recycled_images, coupling_inverse)
+    )(*operands)
+    return pl.pallas_call(
+        combine,
+        out_shape=[jax.ShapeDtypeStruct(residual.shape, f32)] * 3,
+        in_specs=[vmem] * 3,
+        out_specs=[vmem] * 3,
+        compiler_params=pltpu.CompilerParams(vmem_limit_bytes=16 * 2**20),
+        name="combine",
+    )(basis, recycled, coord)
 
 
 def solution(mesh):

time: 73.9 us -> 59.2 us (0.80)
  Pallas kernels: 69.8 us -> 58.3 us
  local copies, waits for them, and re-layouts: 3.21 us -> 0.01 us
    pallas_call x1 -> x2, Pallas kernels: 69.8 us -> 58.3 us  [the longest x1 57.2 us: body(): pl.pallas_call(kernel, out_shape=[jax.ShapeDtypeStruct((NB,) + residual.s...]
    unnamed x7 -> x2, local copies, waits for them, and re-layouts: 3.21 us -> 0.01 us
where the time goes in v2:
time: 59.2 us; the launch traced here: 59 us
  Pallas kernels  58.3 us (98%)
  between operations  0.66 us (1%)
    pallas_call x1, Pallas kernels, body(): pl.pallas_call(kernel, out_shape=[jax.ShapeDtypeStruct((NB,) + residual.s...  57.2 us

profile of v2, /device:TPU:16, one launch (start us, length us, event | category | flops | bytes accessed | tf_op | source)
XLA Modules:
  0.0 59.0 jit_solution(3674427754220425393)
XLA Ops:
  0.6 0.0 copy-start
  0.6 57.2 %block.1 = (f32[9,8,32,128]{3,2,1,0:T(8,128)S(1)}, f32[64,128]{1,0:T(8,128)S(1)}) custom-call(f32[8,32,128]{2,1,0:T(8,128)} %dir_h.1, f32[8,32,128]{2,1,0:T(8,128)} %res_h.1, f32[8,32,128]{2,1,0:T(8,128)} %diag_h.1, bf16[16,8,32,128]{3,2,1,0:T(8,128)(2,1)} %img_h.1, f32[16,16]{1,0:T(8,128)} %c_ref.1), custom_call_target="tpu_custom_call" | custom-call | tf_op jit(solution)/shard_map/block/pallas_call | solution.py:379
  57.9 0.0 copy-done
  57.9 1.1 %combine.1 = (f32[8,32,128]{2,1,0:T(8,128)}, f32[8,32,128]{2,1,0:T(8,128)}, f32[8,32,128]{2,1,0:T(8,128)}) custom-call(f32[9,8,32,128]{3,2,1,0:T(8,128)S(1)} %get-tuple-element.5.basis, bf16[16,8,32,128]{3,2,1,0:T(8,128)(2,1)S(1)} %copy-done, f32[64,128]{1,0:T(8,128)S(1)} %get-tuple-element.6.coord), custom_call_target="tpu_custom_call" | custom-call | tf_op jit(solution)/shard_map/combine/pallas_call | solution.py:414
Async XLA Ops:
  0.6 57.3 %copy-start = (bf16[16,8,32,128]{3,2,1,0:T(8,128)(2,1)S(1)}, bf16[16,8,32,128]{3,2,1,0:T(8,128)(2,1)}, u32[]{:S(2)}) copy-start(bf16[16,8,32,128]{3,2,1,0:T(8,128)(2,1)} %rec.1) | copy-start | bytes 3145732

commit v3 on v2

--- a/solution.py
+++ b/solution.py
@@ -15,27 +15,26 @@
 NR = 16
 
 
+CORNER = ((DIR0, 1, 3, 0), (DIR0, 2, 2, 3), (DIR0, 3, 1, 5), (RES0, 1, 2, 6), (RES0, 2, 1, 8), (DIAG, 1, 2, 9), (DIAG, 2, 1, 11))
+BORDER_CORNER = ((DIR0, 1, 2, 0), (DIR0, 2, 1, 2), (RES0, 1, 1, 3), (DIAG, 1, 1, 4))
+
+
 def rolled(value, shift, axis):
     size = value.shape[axis]
     shift = shift % size
     return pltpu.roll(value, shift, axis) if shift else value
 
 
-def kernel(
-    dir_h, res_h, diag_h, img_h, c_ref,
-    basis_out, coord_out,
-    fld, edge, rnd, img_v,
+def halo(
+    dir_h, res_h, diag_h,
+    fld, edge,
     strip, strip_low, strip_high, merged,
     tile_send, tile_low, tile_high,
-    sums, buf_zc, buf_y, buf_x,
-    local_sem, out_sem, send_sem, recv_sem, zc_send, zc_recv, y_send, y_recv, x_send, x_recv,
+    corner_send, corner_recv, border_send, border_recv,
+    local_sem, send_sem, recv_sem,
 ):
     nx, ny, nz = lax.axis_size("gx"), lax.axis_size("gy"), lax.axis_size("gz")
-    half = nx // 2
     gx, gy, gz = lax.axis_index("gx"), lax.axis_index("gy"), lax.axis_index("gz")
-    col = lax.rem(gx, half)
-    block = gx - col
-    me_zc = lax.div(gx, half) * ny + gy
     x_up = (lax.rem(gx + 1, nx), gy, gz)
     x_down = (lax.rem(gx + nx - 1, nx), gy, gz)
     y_up = (gx, lax.rem(gy + 1, ny), gz)
@@ -43,31 +42,20 @@
     z_up = (gx, gy, lax.rem(gz + 1, nz))
     z_down = (gx, gy, lax.rem(gz + nz - 1, nz))
 
-    def zc_peer(offset):
-        peer = lax.rem(me_zc + offset, 2 * ny)
-        return peer, (lax.div(peer, ny) * half + col, lax.rem(peer, ny), gz)
-
-    def y_peer(offset):
-        peer = lax.rem(col + offset, half)
-        return peer, (block + peer, gy, gz)
-
-    def x_peer(offset):
-        peer = lax.rem(gz + offset, nz)
-        return peer, (gx, gy, peer)
+    corners = [(a, b) for a in (1, -1) for b in (1, -1)]
+
+    def beside(a, b):
+        return (lax.rem(gx + a + nx, nx), lax.rem(gy + b + ny, ny), gz)
 
     sources = (dir_h, res_h, diag_h)
     locals_ = []
     for i, src in enumerate(sources):
         locals_.append(pltpu.make_async_copy(src, fld.at[i, LOW:LOW + 8, ROW:ROW + 32], local_sem.at[i]))
-    locals_.append(pltpu.make_async_copy(img_h, img_v, local_sem.at[3]))
     for copy in locals_:
         copy.start()
 
     barrier = pltpu.get_barrier_semaphore()
-    greeted = [x_up, x_down, y_up, y_down, z_up, z_down]
-    greeted += [zc_peer(o)[1] for o in range(1, 2 * ny)]
-    greeted += [y_peer(o)[1] for o in range(1, half)]
-    greeted += [x_peer(o)[1] for o in range(1, nz)]
+    greeted = [x_up, x_down, y_up, y_down, z_up, z_down] + [beside(a, b) for a, b in corners]
     for device in greeted:
         pl.semaphore_signal(barrier, inc=1, device_id=device, device_id_type=MESH)
     pl.semaphore_wait(barrier, len(greeted))
@@ -93,8 +81,24 @@
         y_copies.append(send(src.at[:, 24:32], fld.at[i, LOW:LOW + 8, ROW - 8:ROW], y_up))
         y_copies.append(send(src.at[:, 0:8], fld.at[i, LOW:LOW + 8, ROW + 32:ROW + 40], y_down))
 
-    for copy in locals_[:3]:
+    for copy in locals_:
         copy.wait()
+
+    def pack_corner(ref, parts, a, b, tile, n):
+        for plane, out, rows, at in parts:
+            x = LOW + 8 - out if a == 1 else LOW + out - 1
+            y = ROW + 32 - rows if b == 1 else ROW
+            tile[n, at:at + rows, :] = ref[plane, x, y:y + rows, :]
+
+    def unpack_corner(ref, parts, a, b, tile, n):
+        for plane, out, rows, at in parts:
+            x = LOW - out if a == 1 else LOW + 7 + out
+            y = ROW - rows if b == 1 else ROW + 32
+            ref[plane, x, y:y + rows, :] = tile[n, at:at + rows, :]
+
+    for n, (a, b) in enumerate(corners):
+        pack_corner(fld, CORNER, a, b, corner_send, n)
+    corner_copies = [send(corner_send.at[n], corner_recv.at[n], beside(a, b)) for n, (a, b) in enumerate(corners)]
 
     lane8 = lax.broadcasted_iota(jnp.int32, (8, 128), 1)
     group8 = lane8 // 8
@@ -118,27 +122,10 @@
     x_copies.append(send(merged.at[:, 2], merged.at[:, 0], x_up))
     x_copies.append(send(merged.at[:, 1], merged.at[:, 3], x_down))
 
-    def place(b):
-        for i in range(3):
-            value = merged[i, b]
-            for q in range(16):
-                t, x = q // 4, q % 4
-                edge[i, 4 * b + x, ROW + 8 * t:ROW + 8 * t + 8, :] = rolled(value, -8 * q - 4, 1)
-
-    place(1)
-    place(2)
-    for copy in x_copies:
-        copy.wait()
-
-    for i, depth in ((0, 3), (1, 2), (2, 2)):
-        for first in (LOW - depth, LOW + 8):
-            layers = slice(first, first + depth)
-            y_copies.append(send(fld.at[i, layers, ROW + 24:ROW + 32], fld.at[i, layers, ROW - 8:ROW], y_up))
-            y_copies.append(send(fld.at[i, layers, ROW:ROW + 8], fld.at[i, layers, ROW + 32:ROW + 40], y_down))
     for i in range(3):
         last = jnp.zeros((8, 128), jnp.float32)
         first = jnp.zeros((8, 128), jnp.float32)
-        for b in range(4):
+        for b in range(1, 3):
             here = (lane8 // 32) == b
             value = merged[i, b]
             last = jnp.where(here, rolled(value, 32 * b - 96, 1), last)
@@ -148,15 +135,92 @@
     y_copies.append(send(tile_send.at[0], tile_low, y_up))
     y_copies.append(send(tile_send.at[1], tile_high, y_down))
 
-    place(0)
-    place(3)
+    def place(b):
+        for i in range(3):
+            value = merged[i, b]
+            for q in range(16):
+                t, x = q // 4, q % 4
+                edge[i, 4 * b + x, ROW + 8 * t:ROW + 8 * t + 8, :] = rolled(value, -8 * q - 4, 1)
+
+    place(1)
+    place(2)
+    for n, (a, b) in enumerate(corners):
+        pack_corner(edge, BORDER_CORNER, a, b, border_send, n)
+    border_copies = [send(border_send.at[n], border_recv.at[n], beside(a, b)) for n, (a, b) in enumerate(corners)]
+
     for copy in y_copies:
         copy.wait()
     for i in range(3):
         low, high = tile_low[i], tile_high[i]
-        for x in range(16):
+        for x in range(4, 12):
             edge[i, x, ROW - 8:ROW, :] = rolled(low, -8 * x - 4, 1)
             edge[i, x, ROW + 32:ROW + 40, :] = rolled(high, -8 * x - 4, 1)
+    for copy in x_copies:
+        copy.wait()
+    place(0)
+    place(3)
+    for copy in corner_copies + border_copies:
+        copy.wait()
+    for n, (a, b) in enumerate(corners):
+        unpack_corner(fld, CORNER, a, b, corner_recv, n)
+        unpack_corner(edge, BORDER_CORNER, a, b, border_recv, n)
+
+
+def block(
+    fld_in, edge_in, img_h, c_ref,
+    basis_out, coord_out,
+    fld_new, edge_new, rnd, img_v,
+    sums, buf_zc, buf_y, buf_x,
+    local_sem, out_sem, zc_send, zc_recv, y_send, y_recv, x_send, x_recv,
+):
+    nx, ny, nz = lax.axis_size("gx"), lax.axis_size("gy"), lax.axis_size("gz")
+    half = nx // 2
+    gx, gy, gz = lax.axis_index("gx"), lax.axis_index("gy"), lax.axis_index("gz")
+    col = lax.rem(gx, half)
+    first_col = gx - col
+    me_zc = lax.div(gx, half) * ny + gy
+
+    def zc_peer(offset):
+        peer = lax.rem(me_zc + offset, 2 * ny)
+        return peer, (lax.div(peer, ny) * half + col, lax.rem(peer, ny), gz)
+
+    def y_peer(offset):
+        peer = lax.rem(col + offset, half)
+        return peer, (first_col + peer, gy, gz)
+
+    def x_peer(offset):
+        peer = lax.rem(gz + offset, nz)
+        return peer, (gx, gy, peer)
+
+    barrier = pltpu.get_barrier_semaphore()
+    greeted = [zc_peer(o)[1] for o in range(1, 2 * ny)]
+    greeted += [y_peer(o)[1] for o in range(1, half)]
+    greeted += [x_peer(o)[1] for o in range(1, nz)]
+    for device in greeted:
+        pl.semaphore_signal(barrier, inc=1, device_id=device, device_id_type=MESH)
+    images_copy = pltpu.make_async_copy(img_h, img_v, local_sem.at[0])
+    images_copy.start()
+
+    class Planes:
+        def __init__(self, given, new):
+            self.given, self.new = given, new
+
+        def of(self, plane):
+            return (self.given, plane) if plane < 3 else (self.new, plane - 3)
+
+        def __getitem__(self, index):
+            ref, plane = self.of(index[0])
+            return ref[(plane,) + index[1:]]
+
+        def __setitem__(self, index, value):
+            ref, plane = self.of(index[0])
+            ref[(plane,) + index[1:]] = value
+
+        def own(self, plane):
+            ref, plane = self.of(plane)
+            return ref.at[plane, LOW:LOW + 8, ROW:ROW + 32]
+
+    fld, edge = Planes(fld_in, fld_new), Planes(edge_in, edge_new)
 
     def apply(mine, other, into, current, earlier, first, last, top, bottom):
         lane = lax.broadcasted_iota(jnp.int32, (bottom - top, 128), 1)
@@ -187,7 +251,7 @@
 
     def put_out(plane):
         j = BASIS.index(plane)
-        copy = pltpu.make_async_copy(fld.at[plane, LOW:LOW + 8, ROW:ROW + 32], basis_out.at[j], out_sem.at[j])
+        copy = pltpu.make_async_copy(fld.own(plane), basis_out.at[j], out_sem.at[j])
         copy.start()
         basis_copies.append(copy)
 
@@ -230,7 +294,7 @@
     gram_pass([(i, j) for i in range(3) for j in range(i, NB)], True)
     gram_pass([(i, j) for i in range(3, NB) for j in range(i, NB)], False)
 
-    locals_[3].wait()
+    images_copy.wait()
 
     @pl.loop(0, NR // 2)
     def _(pair):
@@ -249,13 +313,15 @@
         totals = lax.fori_loop(0, 4, projection_step, (zero,) * (2 * NB))
         for j in range(NB):
             for m in range(2):
-                sums[pl.ds(128 + 16 * j + 2 * pair + m, 1), :] = jnp.sum(totals[2 * j + m], axis=0, keepdims=True)
+                sums[pl.ds((128 + 16 * j if j < 8 else 96) + 2 * pair + m, 1), :] = jnp.sum(totals[2 * j + m], axis=0, keepdims=True)
 
     packed = lax.dot_general(
         jnp.ones((8, 128), jnp.float32), sums[...], (((1,), (1,)), ((), ())),
         precision=lax.Precision.HIGHEST, preferred_element_type=jnp.float32,
     )
-    own = jnp.concatenate([packed[0:1, 128 * g:128 * g + 128] for g in range(4)], axis=0)
+    own = jnp.concatenate([packed[0:1, 128 * g:128 * g + 128] for g in range(2)], axis=0)
+
+    sent = []
 
     def exchange(value, buf, me, peers, count, sends, recvs):
         buf[pl.ds(me, 1)] = value[None]
@@ -274,10 +340,10 @@
                 src_ref=buf.at[peer], dst_ref=buf.at[peer], send_sem=sends.at[o], recv_sem=recvs.at[peer],
                 device_id=device, device_id_type=MESH,
             ).wait_recv()
-        for copy in copies:
-            copy.wait_send()
+        sent.extend(copies)
         return jnp.sum(buf[...], axis=0)
 
+    pl.semaphore_wait(barrier, len(greeted))
     own = exchange(own, buf_zc, me_zc, zc_peer, 2 * ny, zc_send, zc_recv)
     own = exchange(own, buf_y, col, y_peer, half, y_send, y_recv)
     own = exchange(own, buf_x, gz, x_peer, nz, x_send, x_recv)
@@ -291,7 +357,7 @@
     gram = jnp.where(lane < NB, gram, 0.0)
     proj = jnp.zeros(shape, jnp.float32)
     for j in range(NB):
-        proj = jnp.where(sub == j, jnp.broadcast_to(rolled(own[1 + j // 8:2 + j // 8], -16 * j, 1), shape), proj)
+        proj = jnp.where(sub == j, jnp.broadcast_to(rolled(own[1:2], -16 * j, 1) if j < 8 else rolled(own[0:1], -96, 1), shape), proj)
 
     def among(*which):
         hit = sub == which[0]
@@ -332,6 +398,8 @@
     weights = jnp.broadcast_to(weights.astype(jnp.bfloat16).astype(jnp.float32), (NR, 128))
     for n, vector in enumerate((update, residue, search, weights)):
         coord_out[16 * n:16 * n + 16, :] = vector
+    for copy in sent:
+        copy.wait_send()
     for copy in basis_copies:
         copy.wait()
 
@@ -376,16 +444,12 @@
         pltpu.with_memory_space_constraint(x, pltpu.MemorySpace.HBM)
         for x in (direction, residual, diagonal, recycled_images, coupling_inverse)
     ]
-    basis, coord = pl.pallas_call(
-        kernel,
-        out_shape=[jax.ShapeDtypeStruct((NB,) + residual.shape, f32), jax.ShapeDtypeStruct((64, 128), f32)],
-        in_specs=[anywhere] * 4 + [vmem],
-        out_specs=[anywhere, vmem],
+    fields, borders = pl.pallas_call(
+        halo,
+        out_shape=[jax.ShapeDtypeStruct((3, 16, 64, 128), f32)] * 2,
+        in_specs=[anywhere] * 3,
+        out_specs=[vmem] * 2,
         scratch_shapes=[
-            pltpu.VMEM((10, 16, 64, 128), f32),
-            pltpu.VMEM((10, 16, 64, 128), f32),
-            pltpu.VMEM((NB, 8, 32, 128), f32),
-            pltpu.VMEM(recycled.shape, jnp.bfloat16),
             pltpu.VMEM((3, 2) + tile, f32),
             pltpu.VMEM((3, 2) + tile, f32),
             pltpu.VMEM((3, 2) + tile, f32),
@@ -393,14 +457,33 @@
             pltpu.VMEM((2, 3) + tile, f32),
             pltpu.VMEM((3,) + tile, f32),
             pltpu.VMEM((3,) + tile, f32),
-            pltpu.VMEM((512, 128), f32),
-            pltpu.VMEM((2 * ny, 4, 128), f32),
-            pltpu.VMEM((half, 4, 128), f32),
-            pltpu.VMEM((nz, 4, 128), f32),
-            pltpu.SemaphoreType.DMA((4,)),
-            pltpu.SemaphoreType.DMA((NB,)),
+            pltpu.VMEM((4, 16, 128), f32),
+            pltpu.VMEM((4, 16, 128), f32),
+            pltpu.VMEM((4,) + tile, f32),
+            pltpu.VMEM((4,) + tile, f32),
+            pltpu.SemaphoreType.DMA((3,)),
             pltpu.SemaphoreType.DMA((copies,)),
             pltpu.SemaphoreType.DMA((copies,)),
+        ],
+        compiler_params=pltpu.CompilerParams(collective_id=0, has_side_effects=True, vmem_limit_bytes=16 * 2**20),
+        name="halo",
+    )(*operands[:3])
+    basis, coord = pl.pallas_call(
+        block,
+        out_shape=[jax.ShapeDtypeStruct((NB,) + residual.shape, f32), jax.ShapeDtypeStruct((64, 128), f32)],
+        in_specs=[vmem, vmem, anywhere, vmem],
+        out_specs=[anywhere, vmem],
+        scratch_shapes=[
+            pltpu.VMEM((7, 16, 64, 128), f32),
+            pltpu.VMEM((7, 16, 64, 128), f32),
+            pltpu.VMEM((NB, 8, 32, 128), f32),
+            pltpu.VMEM(recycled.shape, jnp.bfloat16),
+            pltpu.VMEM((256, 128), f32),
+            pltpu.VMEM((2 * ny, 2, 128), f32),
+            pltpu.VMEM((half, 2, 128), f32),
+            pltpu.VMEM((nz, 2, 128), f32),
+            pltpu.SemaphoreType.DMA((1,)),
+            pltpu.SemaphoreType.DMA((NB,)),
             pltpu.SemaphoreType.DMA((2 * ny,)),
             pltpu.SemaphoreType.DMA((2 * ny,)),
             pltpu.SemaphoreType.DMA((half,)),
@@ -408,9 +491,9 @@
             pltpu.SemaphoreType.DMA((nz,)),
             pltpu.SemaphoreType.DMA((nz,)),
         ],
-        compiler_params=pltpu.CompilerParams(collective_id=0, has_side_effects=True, vmem_limit_bytes=24 * 2**20),
+        compiler_params=pltpu.CompilerParams(collective_id=1, has_side_effects=True, vmem_limit_bytes=24 * 2**20),
         name="block",
-    )(*operands)
+    )(fields, borders, *operands[3:])
     return pl.pallas_call(
         combine,
         out_shape=[jax.ShapeDtypeStruct(residual.shape, f32)] * 3,

time: 59.2 us -> 57.9 us (0.978)
  Pallas kernels: 58.3 us -> 57 us
    pallas_call x1 -> x2, Pallas kernels: 57.2 us -> 55.9 us  [the longest x1 29.4 us: body(): pl.pallas_call(halo, out_shape=[jax.ShapeDtypeStruct((3, 16, 64, 128), f3...]
where the time goes in v3:
time: 57.9 us; the launch traced here: 57.7 us
  Pallas kernels  57 us (98%)
  between operations  0.66 us (1%)
    pallas_call x1, Pallas kernels, body(): pl.pallas_call(halo, out_shape=[jax.ShapeDtypeStruct((3, 16, 64, 128), f3...  29.4 us
    pallas_call x1, Pallas kernels, body(): pl.pallas_call(block, out_shape=[jax.ShapeDtypeStruct((NB,) + residual.sh...  26.5 us

profile of v3, /device:TPU:16, one launch (start us, length us, event | category | flops | bytes accessed | tf_op | source)
XLA Modules:
  0.0 57.7 jit_solution(7635545674154658873)
XLA Ops:
  0.6 29.4 %halo.1 = (f32[3,16,64,128]{3,2,1,0:T(8,128)S(1)}, f32[3,16,64,128]{3,2,1,0:T(8,128)S(1)}) custom-call(f32[8,32,128]{2,1,0:T(8,128)} %dir_h.1, f32[8,32,128]{2,1,0:T(8,128)} %res_h.1, f32[8,32,128]{2,1,0:T(8,128)} %diag_h.1), custom_call_target="tpu_custom_call" | custom-call | tf_op jit(solution)/shard_map/halo/pallas_call | solution.py:447
  30.1 0.0 copy-start
  30.1 26.5 %block.1 = (f32[9,8,32,128]{3,2,1,0:T(8,128)S(1)}, f32[64,128]{1,0:T(8,128)S(1)}) custom-call(f32[3,16,64,128]{3,2,1,0:T(8,128)S(1)} %get-tuple-element.7.fld_in, f32[3,16,64,128]{3,2,1,0:T(8,128)S(1)} %get-tuple-element.8.edge_in, bf16[16,8,32,128]{3,2,1,0:T(8,128)(2,1)} %img_h.1, f32[16,16]{1,0:T(8,128)} %c_ref.1), custom_call_target="tpu_custom_call" | custom-call | tf_op jit(solution)/shard_map/block/pallas_call | solution.py:471
  56.6 0.0 copy-done
  56.6 1.1 %combine.1 = (f32[8,32,128]{2,1,0:T(8,128)}, f32[8,32,128]{2,1,0:T(8,128)}, f32[8,32,128]{2,1,0:T(8,128)}) custom-call(f32[9,8,32,128]{3,2,1,0:T(8,128)S(1)} %get-tuple-element.9.basis, bf16[16,8,32,128]{3,2,1,0:T(8,128)(2,1)S(1)} %copy-done, f32[64,128]{1,0:T(8,128)S(1)} %get-tuple-element.10.coord), custom_call_target="tpu_custom_call" | custom-call | tf_op jit(solution)/shard_map/combine/pallas_call | solution.py:497
Async XLA Ops:
  30.1 26.5 %copy-start = (bf16[16,8,32,128]{3,2,1,0:T(8,128)(2,1)S(1)}, bf16[16,8,32,128]{3,2,1,0:T(8,128)(2,1)}, u32[]{:S(2)}) copy-start(bf16[16,8,32,128]{3,2,1,0:T(8,128)(2,1)} %rec.1) | copy-start | bytes 3145732

commit v4 on v3

--- a/solution.py
+++ b/solution.py
@@ -30,8 +30,8 @@
     fld, edge,
     strip, strip_low, strip_high, merged,
     tile_send, tile_low, tile_high,
-    corner_send, corner_recv, border_send, border_recv,
-    local_sem, send_sem, recv_sem,
+    corner_send, corner_recv, border_send, border_recv, hop,
+    local_sem, hop_sem, send_sem, recv_sem,
 ):
     nx, ny, nz = lax.axis_size("gx"), lax.axis_size("gy"), lax.axis_size("gz")
     gx, gy, gz = lax.axis_index("gx"), lax.axis_index("gy"), lax.axis_index("gz")
@@ -42,6 +42,11 @@
     z_up = (gx, gy, lax.rem(gz + 1, nz))
     z_down = (gx, gy, lax.rem(gz + nz - 1, nz))
 
+    half = nx // 2
+    col = lax.rem(gx, half)
+    across = half - (gx - col)
+    via = (across + jnp.where(col < 2, col + half - 2, col - (half - 2)), gy, gz)
+    takes_part = jnp.logical_or(col < 2, col >= half - 2)
     corners = [(a, b) for a in (1, -1) for b in (1, -1)]
 
     def beside(a, b):
@@ -58,22 +63,59 @@
     greeted = [x_up, x_down, y_up, y_down, z_up, z_down] + [beside(a, b) for a, b in corners]
     for device in greeted:
         pl.semaphore_signal(barrier, inc=1, device_id=device, device_id_type=MESH)
-    pl.semaphore_wait(barrier, len(greeted))
+
+    @pl.when(takes_part)
+    def _():
+        pl.semaphore_signal(barrier, inc=1, device_id=via, device_id_type=MESH)
+        pl.semaphore_wait(barrier, len(greeted) + 1)
+
+    @pl.when(jnp.logical_not(takes_part))
+    def _():
+        pl.semaphore_wait(barrier, len(greeted))
 
     used = [0]
 
-    def send(src, dst, device):
+    def prepare(src, dst, device):
         i = used[0]
         used[0] += 1
         copy = pltpu.make_async_remote_copy(
             src_ref=src, dst_ref=dst, send_sem=send_sem.at[i], recv_sem=recv_sem.at[i],
             device_id=device, device_id_type=MESH,
         )
+        return copy
+
+    def send(src, dst, device):
+        copy = prepare(src, dst, device)
         copy.start()
         return copy
 
     x_copies = []
-    for i, (src, depth) in enumerate(zip(sources, (4, 3, 3))):
+    passed_on = []
+    for sign, layers, into, device in ((1, diag_h.at[5:8], fld.at[DIAG, LOW - 3:LOW, ROW:ROW + 32], x_up),
+                                       (-1, diag_h.at[0:3], fld.at[DIAG, LOW + 8:LOW + 11, ROW:ROW + 32], x_down)):
+        i = used[0]
+        straight = prepare(layers, into, device)
+        aside = pltpu.make_async_remote_copy(
+            src_ref=layers, dst_ref=hop, send_sem=send_sem.at[i], recv_sem=hop_sem.at[0],
+            device_id=via, device_id_type=MESH,
+        )
+        at_end = col == (half - 1 if sign == 1 else 0)
+
+        @pl.when(at_end)
+        def _():
+            aside.start()
+
+        @pl.when(jnp.logical_not(at_end))
+        def _():
+            straight.start()
+
+        onward = pltpu.make_async_remote_copy(
+            src_ref=hop, dst_ref=into, send_sem=hop_sem.at[1], recv_sem=recv_sem.at[i],
+            device_id=x_down if sign == 1 else x_up, device_id_type=MESH,
+        )
+        x_copies.append(straight)
+        passed_on.append((col == (1 if sign == 1 else half - 2), aside, onward))
+    for i, (src, depth) in enumerate(zip(sources, (4, 3))):
         x_copies.append(send(src.at[8 - depth:8], fld.at[i, LOW - depth:LOW, ROW:ROW + 32], x_up))
         x_copies.append(send(src.at[0:depth], fld.at[i, LOW + 8:LOW + 8 + depth, ROW:ROW + 32], x_down))
     y_copies = []
@@ -147,6 +189,12 @@
     for n, (a, b) in enumerate(corners):
         pack_corner(edge, BORDER_CORNER, a, b, border_send, n)
     border_copies = [send(border_send.at[n], border_recv.at[n], beside(a, b)) for n, (a, b) in enumerate(corners)]
+
+    for here, aside, onward in passed_on:
+        @pl.when(here)
+        def _():
+            aside.wait_recv()
+            onward.start()
 
     for copy in y_copies:
         copy.wait()
@@ -161,6 +209,11 @@
     place(3)
     for copy in corner_copies + border_copies:
         copy.wait()
+    for here, aside, onward in passed_on:
+        @pl.when(here)
+        def _():
+            onward.wait_send()
+
     for n, (a, b) in enumerate(corners):
         unpack_corner(fld, CORNER, a, b, corner_recv, n)
         unpack_corner(edge, BORDER_CORNER, a, b, border_recv, n)
@@ -461,7 +514,9 @@
             pltpu.VMEM((4, 16, 128), f32),
             pltpu.VMEM((4,) + tile, f32),
             pltpu.VMEM((4,) + tile, f32),
+            pltpu.VMEM((3, 32, 128), f32),
             pltpu.SemaphoreType.DMA((3,)),
+            pltpu.SemaphoreType.DMA((2,)),
             pltpu.SemaphoreType.DMA((copies,)),
             pltpu.SemaphoreType.DMA((copies,)),
         ],

time: 57.9 us -> 56.3 us (0.972)
  Pallas kernels: 57 us -> 55.4 us
    pallas_call x1, Pallas kernels: 26.5 us -> 24.7 us  [body(): pl.pallas_call(block, out_shape=[jax.ShapeDtypeStruct((NB,) + residual.sh...]
where the time goes in v4:
time: 56.3 us; the launch traced here: 56.1 us
  Pallas kernels  55.4 us (98%)
  between operations  0.66 us (1%)
    pallas_call x1, Pallas kernels, body(): pl.pallas_call(halo, out_shape=[jax.ShapeDtypeStruct((3, 16, 64, 128), f3...  29.6 us
    pallas_call x1, Pallas kernels, body(): pl.pallas_call(block, out_shape=[jax.ShapeDtypeStruct((NB,) + residual.sh...  24.7 us

profile of v4, /device:TPU:16, one launch (start us, length us, event | category | flops | bytes accessed | tf_op | source)
XLA Modules:
  0.0 56.1 jit_solution(10816148946106330913)
XLA Ops:
  0.6 29.6 %halo.1 = (f32[3,16,64,128]{3,2,1,0:T(8,128)S(1)}, f32[3,16,64,128]{3,2,1,0:T(8,128)S(1)}) custom-call(f32[8,32,128]{2,1,0:T(8,128)} %dir_h.1, f32[8,32,128]{2,1,0:T(8,128)} %res_h.1, f32[8,32,128]{2,1,0:T(8,128)} %diag_h.1), custom_call_target="tpu_custom_call" | custom-call | tf_op jit(solution)/shard_map/halo/pallas_call | solution.py:500
  30.3 0.0 copy-start
  30.3 24.7 %block.1 = (f32[9,8,32,128]{3,2,1,0:T(8,128)S(1)}, f32[64,128]{1,0:T(8,128)S(1)}) custom-call(f32[3,16,64,128]{3,2,1,0:T(8,128)S(1)} %get-tuple-element.7.fld_in, f32[3,16,64,128]{3,2,1,0:T(8,128)S(1)} %get-tuple-element.8.edge_in, bf16[16,8,32,128]{3,2,1,0:T(8,128)(2,1)} %img_h.1, f32[16,16]{1,0:T(8,128)} %c_ref.1), custom_call_target="tpu_custom_call" | custom-call | tf_op jit(solution)/shard_map/block/pallas_call | solution.py:526
  55.0 0.0 copy-done
  55.0 1.1 %combine.1 = (f32[8,32,128]{2,1,0:T(8,128)}, f32[8,32,128]{2,1,0:T(8,128)}, f32[8,32,128]{2,1,0:T(8,128)}) custom-call(f32[9,8,32,128]{3,2,1,0:T(8,128)S(1)} %get-tuple-element.9.basis, bf16[16,8,32,128]{3,2,1,0:T(8,128)(2,1)S(1)} %copy-done, f32[64,128]{1,0:T(8,128)S(1)} %get-tuple-element.10.coord), custom_call_target="tpu_custom_call" | custom-call | tf_op jit(solution)/shard_map/combine/pallas_call | solution.py:552
Async XLA Ops:
  30.3 24.7 %copy-start = (bf16[16,8,32,128]{3,2,1,0:T(8,128)(2,1)S(1)}, bf16[16,8,32,128]{3,2,1,0:T(8,128)(2,1)}, u32[]{:S(2)}) copy-start(bf16[16,8,32,128]{3,2,1,0:T(8,128)(2,1)} %rec.1) | copy-start | bytes 3145732

commit v5 on v4

--- a/solution.py
+++ b/solution.py
@@ -138,10 +138,6 @@
             y = ROW - rows if b == 1 else ROW + 32
             ref[plane, x, y:y + rows, :] = tile[n, at:at + rows, :]
 
-    for n, (a, b) in enumerate(corners):
-        pack_corner(fld, CORNER, a, b, corner_send, n)
-    corner_copies = [send(corner_send.at[n], corner_recv.at[n], beside(a, b)) for n, (a, b) in enumerate(corners)]
-
     lane8 = lax.broadcasted_iota(jnp.int32, (8, 128), 1)
     group8 = lane8 // 8
 
@@ -155,6 +151,9 @@
             strip[i, h] = packed
 
     z_copies = [send(strip, strip_low, z_up), send(strip, strip_high, z_down)]
+    for n, (a, b) in enumerate(corners):
+        pack_corner(fld, CORNER, a, b, corner_send, n)
+    corner_copies = [send(corner_send.at[n], corner_recv.at[n], beside(a, b)) for n, (a, b) in enumerate(corners)]
     for copy in z_copies:
         copy.wait()
     from_low = lane8 % 8 < 4

time: 56.3 us -> 56.3 us (level)
  no operation moved by 1% of the time
where the time goes in v5:
time: 56.3 us; the launch traced here: 56.1 us
  Pallas kernels  55.4 us (98%)
  between operations  0.66 us (1%)
    pallas_call x1, Pallas kernels, body(): pl.pallas_call(halo, out_shape=[jax.ShapeDtypeStruct((3, 16, 64, 128), f3...  29.6 us
    pallas_call x1, Pallas kernels, body(): pl.pallas_call(block, out_shape=[jax.ShapeDtypeStruct((NB,) + residual.sh...  24.7 us

profile of v5, /device:TPU:16, one launch (start us, length us, event | category | flops | bytes accessed | tf_op | source)
XLA Modules:
  0.0 56.1 jit_solution(13629783434105613593)
XLA Ops:
  0.6 29.6 %halo.1 = (f32[3,16,64,128]{3,2,1,0:T(8,128)S(1)}, f32[3,16,64,128]{3,2,1,0:T(8,128)S(1)}) custom-call(f32[8,32,128]{2,1,0:T(8,128)} %dir_h.1, f32[8,32,128]{2,1,0:T(8,128)} %res_h.1, f32[8,32,128]{2,1,0:T(8,128)} %diag_h.1), custom_call_target="tpu_custom_call" | custom-call | tf_op jit(solution)/shard_map/halo/pallas_call | solution.py:499
  30.3 0.0 copy-start
  30.3 24.7 %block.1 = (f32[9,8,32,128]{3,2,1,0:T(8,128)S(1)}, f32[64,128]{1,0:T(8,128)S(1)}) custom-call(f32[3,16,64,128]{3,2,1,0:T(8,128)S(1)} %get-tuple-element.7.fld_in, f32[3,16,64,128]{3,2,1,0:T(8,128)S(1)} %get-tuple-element.8.edge_in, bf16[16,8,32,128]{3,2,1,0:T(8,128)(2,1)} %img_h.1, f32[16,16]{1,0:T(8,128)} %c_ref.1), custom_call_target="tpu_custom_call" | custom-call | tf_op jit(solution)/shard_map/block/pallas_call | solution.py:525
  55.0 0.0 copy-done
  55.0 1.1 %combine.1 = (f32[8,32,128]{2,1,0:T(8,128)}, f32[8,32,128]{2,1,0:T(8,128)}, f32[8,32,128]{2,1,0:T(8,128)}) custom-call(f32[9,8,32,128]{3,2,1,0:T(8,128)S(1)} %get-tuple-element.9.basis, bf16[16,8,32,128]{3,2,1,0:T(8,128)(2,1)S(1)} %copy-done, f32[64,128]{1,0:T(8,128)S(1)} %get-tuple-element.10.coord), custom_call_target="tpu_custom_call" | custom-call | tf_op jit(solution)/shard_map/combine/pallas_call | solution.py:551
Async XLA Ops:
  30.3 24.7 %copy-start = (bf16[16,8,32,128]{3,2,1,0:T(8,128)(2,1)S(1)}, bf16[16,8,32,128]{3,2,1,0:T(8,128)(2,1)}, u32[]{:S(2)}) copy-start(bf16[16,8,32,128]{3,2,1,0:T(8,128)(2,1)} %rec.1) | copy-start | bytes 3145732
